TPU v7x, 32 devices: a whole 2x2x4 slice. The times are simulated.
32 devices in a mesh: ctx: 8 (over z, y), tp: 4 (over x, core).
Axes of the slice: x: 2, y: 2, z: 4, core: 2. Of those that a mesh axis runs over, the one named last changes fastest.
Arguments:
- features: bfloat16 [3, 1024, 4096], P(None, 'ctx', 'tp'), may hold values from -6 to 6
- out_grad: bfloat16 [1024, 4096], P('ctx', 'tp'), may hold values from -6 to 6
- attn_parts: bfloat16 [4, 1024, 4096], P('tp', 'ctx'), may hold values from -6 to 6
- short_filt: bfloat16 [3, 256, 7], P(None, 'tp'), may hold values from -2 to 2
- med_filt: bfloat16 [256, 128], P('tp'), may hold values from -0.5 to 0.5
- piece_home: int32 [32], replicated, may hold values from 0 to 7, as said below
- piece_start: int32 [32], replicated, may hold values from 0 to 96, as said below
Outputs:
- feat_grad: bfloat16 [3, 1024, 4096], P(None, 'ctx', 'tp')
- short_grad: float32 [3, 256, 7], P(None, 'tp')
- med_grad: float32 [256, 128], P('tp')
Inputs may be any that keep to these rules, and one draw needn't show every extreme that they name: `piece_home`: entry i * 4 + l names the home device of the piece of 32 rows that starts at row l * 32 of device i in the balanced layout. With piece_start the entries name every piece of every home device exactly once, and no device of the balanced layout holds two pieces of the same home device. `piece_start`: A multiple of 32.
All inputs are finite; a program needn't handle non-finite values.
Results may differ from a plain program's by a relative error of at most 0.012.
Values may be sent and summed in bfloat16 or wider, within the bound.
A program may use at most 64 MiB of HBM per device.

v0:
```python
import math

import jax
import jax.numpy as jnp
from jax import lax
from jax.sharding import PartitionSpec as P

GROUP = 16


def shifted(x, axis, by):
    size = lax.axis_size(axis)
    pairs = [(i, i + by) for i in range(size) if 0 <= i + by < size]
    return lax.ppermute(x, axis, pairs)


def band_table(filt, causal):
    taps = filt.shape[1]
    base = filt[:, ::-1] if causal else filt
    line = jnp.concatenate([base, jnp.zeros_like(base)], axis=1)
    tiled = jnp.tile(line, (1, taps))[:, : taps * (2 * taps - 1)]
    return tiled.reshape(filt.shape[0], taps, 2 * taps - 1)


def band_apply(table, padded):
    taps = table.shape[1]
    groups = table.shape[0]
    width = padded.shape[1]
    window = padded.reshape(2 * taps - 1, groups, width // groups)
    product = jnp.einsum("gtu,ugc->tgc", table, window, preferred_element_type=jnp.float32)
    results = product.reshape(taps, width)
    return results


def lag_products(grads, padded, taps, groups):
    rows = grads.shape[0]
    block_rows = min(rows, 64)
    span = block_rows + taps
    extended = jnp.concatenate([padded, jnp.zeros((1, padded.shape[1]), padded.dtype)], axis=0)
    total = jnp.zeros((groups, taps), jnp.float32)
    for block in range(rows // block_rows):
        first = block * block_rows
        left = grads[first : first + block_rows].reshape(block_rows, groups, -1)
        window = extended[first : first + span].reshape(span, groups, -1)
        cross = jnp.einsum("tgc,ugc->gtu", left, window, preferred_element_type=jnp.float32)
        flat = jnp.pad(cross.reshape(groups, block_rows * span), ((0, 0), (0, block_rows)))
        skewed = flat.reshape(groups, block_rows, span + 1)
        total = total + jnp.sum(skewed[:, :, :taps], axis=1)
    return total[:, ::-1]


def shards(features, out_grad, attn_parts, short_filt, med_filt, piece_home, piece_start):
    rows = out_grad.shape[0]
    width = out_grad.shape[1]
    groups = med_filt.shape[0]
    taps = med_filt.shape[1]
    short_taps = short_filt.shape[2]
    ctx_count = lax.axis_size("ctx")
    own_index = lax.axis_index("ctx")
    per_device = ctx_count // 2
    piece_rows = rows // per_device
    factor = 1.0 / math.sqrt(rows * ctx_count * GROUP)
    everyone = piece_home.reshape(ctx_count, per_device)
    positions = (piece_start // piece_rows).reshape(ctx_count, per_device)
    local_home = lax.dynamic_slice_in_dim(everyone, own_index, 1, 0)[0]
    device_ids = jnp.arange(ctx_count, dtype=jnp.int32)
    slot_ids = jnp.arange(per_device, dtype=jnp.int32)
    matches = local_home[None, :] == device_ids[:, None]
    send_slot = jnp.sum(jnp.where(matches, slot_ids[None, :], 0), axis=1)
    send_live = jnp.any(matches, axis=1)
    keyed = jnp.where(everyone == own_index, positions, -1)
    hits = jnp.any(keyed[:, :, None] == slot_ids[None, None, :], axis=1)
    source_of = jnp.sum(jnp.where(hits, device_ids[:, None], 0), axis=0)
    summed = lax.psum_scatter(
        attn_parts[0].astype(jnp.float32).astype(jnp.bfloat16),
        "tp",
        scatter_dimension=1,
        tiled=True,
    )
    pieces = summed.reshape(per_device, piece_rows, -1)
    attn_home = lax.all_to_all(
        jnp.where(send_live[:, None, None], pieces[send_slot], 0),
        "ctx",
        split_axis=0,
        concat_axis=0,
        tiled=True,
    )[source_of].reshape(rows, -1)
    short_weights = jnp.transpose(jnp.repeat(short_filt, GROUP, axis=1), (0, 2, 1)).astype(
        jnp.float32
    )
    stream_rim = shifted(features[:, rows - short_taps + 1 :, :], "ctx", 1)
    extended = jnp.concatenate([stream_rim, features], axis=1)
    streams = jnp.zeros((3, rows, width), jnp.float32)
    for lag in range(short_taps):
        start = short_taps - 1 - lag
        streams = streams + short_weights[:, lag][:, None, :] * extended[
            :, start : start + rows, :
        ].astype(jnp.float32)
    query, keys, values = (streams[0], streams[1], streams[2])
    keyval = (keys * values).astype(jnp.bfloat16)
    key_rim = shifted(keyval[rows - taps + 1 :], "ctx", 1)
    key_ext = jnp.concatenate([key_rim, keyval], axis=0)
    mixed = band_apply(band_table(med_filt, True), key_ext)
    grad = out_grad.astype(jnp.float32) + attn_home.astype(jnp.float32)
    dquery = grad * mixed
    dmix = (grad * query).astype(jnp.bfloat16)
    back_table = band_table(med_filt, False)
    grad_rim = shifted(dmix[: taps - 1], "ctx", -1)
    dkeyval = band_apply(back_table, jnp.concatenate([dmix, grad_rim], axis=0))
    dstreams = jnp.stack([dquery, dkeyval * values, dkeyval * keys])
    grad_rim_short = shifted(dstreams[:, : short_taps - 1].astype(jnp.bfloat16), "ctx", -1).astype(
        jnp.float32
    )
    grad_ext = jnp.concatenate([dstreams, grad_rim_short], axis=1)
    feat_total = jnp.zeros((3, rows, width), jnp.float32)
    short_columns = []
    for lag in range(short_taps):
        feat_total = (
            feat_total + short_weights[:, lag][:, None, :] * grad_ext[:, lag : lag + rows, :]
        )
        start = short_taps - 1 - lag
        summed = jnp.sum(
            dstreams * extended[:, start : start + rows, :].astype(jnp.float32), axis=1
        )
        short_columns.append(summed.reshape(3, groups, GROUP).sum(axis=2))
    feat_grad = feat_total.astype(jnp.bfloat16)
    short_part = jnp.stack(short_columns, axis=2)
    med_part = lag_products(dmix, key_ext, taps, groups)
    totals = lax.psum((short_part, med_part), "ctx")
    return (feat_grad, totals[0] * factor, totals[1] * factor)


def solution(mesh):
    return jax.shard_map(
        shards,
        mesh=mesh,
        in_specs=(
            P(None, "ctx", "tp"),
            P("ctx", "tp"),
            P("tp", "ctx", None),
            P(None, "tp", None),
            P("tp", None),
            P(),
            P(),
        ),
        out_specs=(P(None, "ctx", "tp"), P(None, "tp", None), P("tp", None)),
        check_vma=False,
    )
```

profile of v0, /device:TPU:0, one launch (start us, length us, event | category | flops | bytes accessed | tf_op | source)
XLA Modules:
  0.0 222.2 jit_solution(5527139569925320712)
XLA Ops:
  7.2 0.7 reduce-scatter.2.cloned.1.call-update
  7.9 0.8 slice.121
  8.7 4.9 %collective-permute-start = (bf16[3,6,1024]{2,1,0:T(8,128)(2,1)S(1)}, bf16[3,6,1024]{2,1,0:T(8,128)(2,1)S(1)}, u32[]{:S(2)}, u32[]{:S(2)}) collective-permute-start(bf16[3,6,1024]{2,1,0:T(8,128)(2,1)S(1)} %slice.121), channel_id=1, source_target_pairs={{0,4},{4,8},{8,12},{12,16},{16,20},{20,24},{24,28},{1,5},{5,9},{9,... | collective-permute-start | bytes 110600 | tf_op jit(solution)/shard_map/ppermute | solution.py:14
  13.7 0.9 broadcast_in_dim.50
  14.6 0.4 convert_element_type.71
  15.4 0.1 select_reduce_fusion
  15.7 22.4 %reduce-scatter.2.cloned.1.call-done = bf16[128,1024]{1,0:T(8,128)(2,1)} async-done(((bf16[128,4096]{1,0:T(8,128)(2,1)}), bf16[128,1024]{1,0:T(8,128)(2,1)}) %reduce-scatter.2.cloned.1.call-update) | async-done | bytes 262160 | tf_op jit(solution)/shard_map/reduce_scatter | solution.py:74
  38.1 1.6 gather_fusion
  39.7 0.9 broadcast_select_fusion
  40.6 5.5 %all-to-all-start = ((bf16[8,32,1024]{2,1,0:T(8,128)(2,1)}), bf16[8,32,1024]{2,1,0:T(8,128)(2,1)S(1)}, u32[]{:S(2)}, u32[]{:S(2)}) async-start(bf16[8,32,1024]{2,1,0:T(8,128)(2,1)} %broadcast_select_fusion), calls=%async_computation.1 | async-start | bytes 1048576 | tf_op jit(solution)/shard_map/all_to_all | solution.py:81
  46.1 0.6 pad_clamp_fusion
  46.7 1.5 fusion.5
  48.3 12.1 %all-to-all-done = bf16[8,32,1024]{2,1,0:T(8,128)(2,1)S(1)} async-done(((bf16[8,32,1024]{2,1,0:T(8,128)(2,1)}), bf16[8,32,1024]{2,1,0:T(8,128)(2,1)S(1)}, u32[]{:S(2)}, u32[]{:S(2)}) %all-to-all-start) | async-done | bytes 524320 | tf_op jit(solution)/shard_map/all_to_all | solution.py:81
  60.4 0.7 gather_fusion.1
  61.1 0.1 fusion.26
  61.2 1.3 collective-permute-start.2
  62.5 0.3 tile.20
  62.8 2.6 %copy.49 = bf16[8,8,128,256]{3,1,2,0:T(8,128)(2,1)S(1)} copy(bf16[8,8,128,256]{3,2,1,0:T(8,128)(2,1)S(1)} %bitcast.87) | data formatting | bytes 8388608
  65.4 2.2 %slice.181 = bf16[64,32640]{1,0:T(8,128)(2,1)} slice(bf16[64,32768]{1,0:T(8,128)(2,1)S(1)} %bitcast.89), slice={[0:64], [0:32640]} | slice | bytes 8355840 | tf_op jit(solution)/shard_map/slice | solution.py:21
  67.7 15.8 %reshape.140 = bf16[64,128,255]{2,1,0:T(8,128)(2,1)} reshape(bf16[64,32640]{1,0:T(8,128)(2,1)} %slice.181) | data formatting | bytes 8355840 | tf_op jit(solution)/shard_map/reshape | solution.py:22
  83.6 0.2 copy.33
  83.8 3.4 %fusion.36 = f32[64,16,128]{2,1,0:T(8,128)S(1)} fusion(bf16[255,64,16]{0,2,1:T(8,128)(2,1)S(1)} %bitcast.96, bf16[64,128,255]{2,1,0:T(8,128)(2,1)} %reshape.140), kind=kOutput, calls=%fused_computation.112 | convolution fusion | flops 66846720 | bytes 5224448 | tf_op jit(solution)/shard_map/gtu,ugc->tgc/dot_general | solution.py:30
  87.1 1.0 copy.34
  88.2 1.2 slice_multiply_fusion.6
  89.4 4.7 %collective-permute-start.1 = (bf16[127,1024]{1,0:T(8,128)(2,1)S(1)}, bf16[127,1024]{1,0:T(8,128)(2,1)S(1)}, u32[]{:S(2)}, u32[]{:S(2)}) collective-permute-start(bf16[127,1024]{1,0:T(8,128)(2,1)S(1)} %slice_bitcast_fusion.1), channel_id=1, source_target_pairs={{0,4},{4,8},{8,12},{12,16},{16,20},{20,24},{24,28},{1,5},{5,9},{9,... | collective-permute-start | bytes 780296 | tf_op jit(solution)/shard_map/ppermute | solution.py:14
  94.2 0.8 rev.6
  95.0 0.6 slice.194
  95.6 0.3 tile.8
  95.9 2.6 %copy.48 = bf16[8,8,128,256]{3,1,2,0:T(8,128)(2,1)S(1)} copy(bf16[8,8,128,256]{3,2,1,0:T(8,128)(2,1)S(1)} %bitcast.88) | data formatting | bytes 8388608
  98.5 2.2 %slice.178 = bf16[64,32640]{1,0:T(8,128)(2,1)} slice(bf16[64,32768]{1,0:T(8,128)(2,1)S(1)} %bitcast.90), slice={[0:64], [0:32640]} | slice | bytes 8355840 | tf_op jit(solution)/shard_map/slice | solution.py:21
  100.8 15.8 %reshape.137 = bf16[64,128,255]{2,1,0:T(8,128)(2,1)} reshape(bf16[64,32640]{1,0:T(8,128)(2,1)} %slice.178) | data formatting | bytes 8355840 | tf_op jit(solution)/shard_map/reshape | solution.py:22
  116.6 0.2 copy.38
  116.8 0.2 copy.36
  117.0 0.8 fusion.28
  117.9 0.2 copy.39
  118.1 2.7 %fusion.38 = f32[64,64,192]{2,1,0:T(8,128)} fusion(bf16[64,64,16]{0,2,1:T(8,128)(2,1)S(1)} %bitcast.101, bf16[192,64,16]{0,2,1:T(8,128)(2,1)S(1)} %bitcast.94), kind=kOutput, calls=%fused_computation.114 | convolution fusion | flops 25165824 | bytes 3670016 | tf_op jit(solution)/shard_map/tgc,ugc->gtu/dot_general | solution.py:45
  120.8 5.2 %reshape.155 = f32[64,12288]{1,0:T(8,128)} reshape(f32[64,64,192]{2,1,0:T(8,128)} %fusion.38) | data formatting | bytes 6291456 | tf_op jit(solution)/shard_map/reshape | solution.py:46
  126.0 3.9 %pad.10 = f32[64,12352]{1,0:T(8,128)} pad(f32[64,12288]{1,0:T(8,128)} %reshape.155, f32[]{:T(128)} %constant.41.clone.1), padding=0_0x0_64 | pad | bytes 6307844 | tf_op jit(solution)/shard_map/jit(_pad)/pad | solution.py:46
  129.9 8.0 %reshape.156 = f32[64,64,193]{2,1,0:T(8,128)} reshape(f32[64,12352]{1,0:T(8,128)} %pad.10) | data formatting | bytes 6324224 | tf_op jit(solution)/shard_map/reshape | solution.py:47
  137.9 1.8 slice_reduce_fusion
  139.8 0.2 copy.37
  140.0 2.7 %fusion.37 = f32[64,64,192]{2,1,0:T(8,128)} fusion(bf16[64,64,16]{0,2,1:T(8,128)(2,1)S(1)} %bitcast.100, bf16[192,64,16]{0,2,1:T(8,128)(2,1)S(1)} %bitcast.95), kind=kOutput, calls=%fused_computation.113 | convolution fusion | flops 25165824 | bytes 3670016 | tf_op jit(solution)/shard_map/tgc,ugc->gtu/dot_general | solution.py:45
  142.7 5.2 %reshape.151 = f32[64,12288]{1,0:T(8,128)} reshape(f32[64,64,192]{2,1,0:T(8,128)} %fusion.37) | data formatting | bytes 6291456 | tf_op jit(solution)/shard_map/reshape | solution.py:46
  147.9 3.9 %pad.9 = f32[64,12352]{1,0:T(8,128)} pad(f32[64,12288]{1,0:T(8,128)} %reshape.151, f32[]{:T(128)} %constant.41.clone.1), padding=0_0x0_64 | pad | bytes 6307844 | tf_op jit(solution)/shard_map/jit(_pad)/pad | solution.py:46
  151.8 8.0 %reshape.152 = f32[64,64,193]{2,1,0:T(8,128)} reshape(f32[64,12352]{1,0:T(8,128)} %pad.9) | data formatting | bytes 6324224 | tf_op jit(solution)/shard_map/reshape | solution.py:47
  159.8 1.9 slice_reduce_fusion.1
  161.9 0.2 copy.31
  162.1 3.4 %fusion.35 = f32[64,16,128]{2,1,0:T(8,128)S(1)} fusion(bf16[255,64,16]{0,2,1:T(8,128)(2,1)S(1)} %bitcast.98, bf16[64,128,255]{2,1,0:T(8,128)(2,1)} %reshape.137), kind=kOutput, calls=%fused_computation.111 | convolution fusion | flops 66846720 | bytes 5224448 | tf_op jit(solution)/shard_map/gtu,ugc->tgc/dot_general | solution.py:30
  165.5 0.2 copy.32
  165.8 0.1 pad_maximum_fusion.1
  166.0 1.0 copy-done.1
  167.0 1.7 fusion.11
  168.8 0.1 reduce_sum.171
  169.0 0.1 reduce_sum.173
  169.2 0.1 reduce_sum.175
  169.4 0.1 reduce_sum.177
  170.2 35.6 %all-reduce.4 = (f32[3,64,7]{1,0,2:T(4,128)S(1)}, f32[64,128]{1,0:T(8,128)S(1)}) all-reduce(f32[3,64,7]{1,0,2:T(4,128)S(1)} %constant_dynamic-update-slice_fusion, f32[64,128]{1,0:T(8,128)S(1)} %rev.7), channel_id=1, replica_groups=mesh['ctx'=8,'tp'=4] {'ctx'}, use_global_device_ids=true, to_apply=%region_19.20 | all-reduce | flops 9536 | bytes 76288 | tf_op jit(solution)/shard_map/psum | solution.py:129
  205.9 0.6 broadcast_multiply_fusion
  206.5 1.3 collective-permute-start.3
  207.8 0.6 copy.40
  208.4 4.1 %collective-permute-done.3 = bf16[3,6,1024]{2,1,0:T(8,128)(2,1)S(1)} collective-permute-done((bf16[3,6,1024]{2,1,0:T(8,128)(2,1)S(1)}, bf16[3,6,1024]{2,1,0:T(8,128)(2,1)S(1)}, u32[]{:S(2)}, u32[]{:S(2)}) %collective-permute-start.3) | collective-permute-done | bytes 36896 | tf_op jit(solution)/shard_map/ppermute | solution.py:14
  212.5 0.2 pad_maximum_fusion
  212.7 0.5 copy-done.7
  213.2 2.2 fusion.14
  (71 shorter events, 2.2 us)
Async XLA Ops:
  7.2 7.8 %copy-start.9 = (s32[32]{0:T(128)S(1)}, s32[32]{0:T(128)}, u32[]{:S(2)}) copy-start(s32[32]{0:T(128)} %param.12) | copy-start | bytes 388
  7.2 7.9 %copy-start.10 = (s32[32]{0:T(128)S(1)}, s32[32]{0:T(128)}, u32[]{:S(2)}) copy-start(s32[32]{0:T(128)} %param.13) | copy-start | bytes 388
  7.2 30.9 %reduce-scatter.2.cloned.1.call-start = ((), (), s32[]{:S(2)}) async-start(), calls=%async_computation.2 | async-start | bytes 1310720 | tf_op jit(solution)/shard_map/reduce_scatter | solution.py:74
  8.7 38.0 %collective-permute-start = (bf16[3,6,1024]{2,1,0:T(8,128)(2,1)S(1)}, bf16[3,6,1024]{2,1,0:T(8,128)(2,1)S(1)}, u32[]{:S(2)}, u32[]{:S(2)}) collective-permute-start(bf16[3,6,1024]{2,1,0:T(8,128)(2,1)S(1)} %slice.121), channel_id=1, source_target_pairs={{0,4},{4,8},{8,12},{12,16},{16,20},{20,24},{24,28},{1,5},{5,9},{9,... | collective-permute-start | bytes 110600 | tf_op jit(solution)/shard_map/ppermute | solution.py:14
  38.1 8.7 %copy-start = (bf16[3,128,1024]{2,1,0:T(8,128)(2,1)S(1)}, bf16[3,128,1024]{2,1,0:T(8,128)(2,1)}, u32[]{:S(2)}) copy-start(bf16[3,128,1024]{2,1,0:T(8,128)(2,1)} %param.7) | copy-start | bytes 2359300
  40.6 19.8 %all-to-all-start = ((bf16[8,32,1024]{2,1,0:T(8,128)(2,1)}), bf16[8,32,1024]{2,1,0:T(8,128)(2,1)S(1)}, u32[]{:S(2)}, u32[]{:S(2)}) async-start(bf16[8,32,1024]{2,1,0:T(8,128)(2,1)} %broadcast_select_fusion), calls=%async_computation.1 | async-start | bytes 1048576 | tf_op jit(solution)/shard_map/all_to_all | solution.py:81
  46.1 15.0 %copy-start.2 = (bf16[128,1024]{1,0:T(8,128)(2,1)S(1)}, bf16[128,1024]{1,0:T(8,128)(2,1)}, u32[]{:S(2)}) copy-start(bf16[128,1024]{1,0:T(8,128)(2,1)} %param.8) | copy-start | bytes 786436
  46.7 1.5 copy-start.6
  48.2 14.3 %copy-start.8 = (bf16[64,128]{1,0:T(8,128)(2,1)S(1)}, bf16[64,128]{1,0:T(8,128)(2,1)}, u32[]{:S(2)}) copy-start(bf16[64,128]{1,0:T(8,128)(2,1)} %param.11) | copy-start | bytes 49156
  61.2 22.3 %collective-permute-start.2 = (bf16[127,1024]{1,0:T(8,128)(2,1)S(1)}, bf16[127,1024]{1,0:T(8,128)(2,1)S(1)}, u32[]{:S(2)}, u32[]{:S(2)}) collective-permute-start(bf16[127,1024]{1,0:T(8,128)(2,1)S(1)} %bitcast.93), channel_id=1, source_target_pairs={{4,0},{8,4},{12,8},{16,12},{20,16},{24,20},{28,24},{5,1},{9,5},{13... | collective-permute-start | bytes 780296 | tf_op jit(solution)/shard_map/ppermute | solution.py:14
  89.4 27.6 %collective-permute-start.1 = (bf16[127,1024]{1,0:T(8,128)(2,1)S(1)}, bf16[127,1024]{1,0:T(8,128)(2,1)S(1)}, u32[]{:S(2)}, u32[]{:S(2)}) collective-permute-start(bf16[127,1024]{1,0:T(8,128)(2,1)S(1)} %slice_bitcast_fusion.1), channel_id=1, source_target_pairs={{0,4},{4,8},{8,12},{12,16},{16,20},{20,24},{24,28},{1,5},{5,9},{9,... | collective-permute-start | bytes 780296 | tf_op jit(solution)/shard_map/ppermute | solution.py:14
  117.0 0.9 copy-start.4
  159.8 2.0 copy-start.5
  162.1 3.6 %copy-start.3 = (bf16[128,1024]{1,0:T(8,128)(2,1)S(1)}, bf16[128,1024]{1,0:T(8,128)(2,1)}, u32[]{:S(2)}) copy-start(bf16[128,1024]{1,0:T(8,128)(2,1)} %param.8) | copy-start | bytes 786436
  165.8 1.1 copy-start.1
  206.5 6.0 %collective-permute-start.3 = (bf16[3,6,1024]{2,1,0:T(8,128)(2,1)S(1)}, bf16[3,6,1024]{2,1,0:T(8,128)(2,1)S(1)}, u32[]{:S(2)}, u32[]{:S(2)}) collective-permute-start(bf16[3,6,1024]{2,1,0:T(8,128)(2,1)S(1)} %slice.305), channel_id=1, source_target_pairs={{4,0},{8,4},{12,8},{16,12},{20,16},{24,20},{28,24},{5,1},{9,5},{13... | collective-permute-start | bytes 110600 | tf_op jit(solution)/shard_map/ppermute | solution.py:14
  212.5 0.7 copy-start.7
Sparse Core Ops, SparseCore 0:
  10.5 27.4 reduce-scatter.1
where the time goes:
time: 223 us; the launch traced here: 222 us
  local copies, waits for them, and re-layouts  87.8 us (39%)
  waiting for transfers between devices  39.3 us (18%)
  blocking collectives  35.6 us (16%)
  starting transfers between devices  17.8 us (8%)
  other arithmetic  14.9 us (7%)
  between operations  14.6 us (7%)
  matrix products  12.2 us (5%)
    psum x1, blocking collectives, shards(): totals = lax.psum((short_part, med_part), 'ctx')  35.6 us
    reshape x2, local copies, waits for them, and re-layouts, band_table(): return tiled.reshape(filt.shape[0], taps, 2 * taps - 1)  31.7 us
    reduce_scatter x1, waiting for transfers between devices, shards(): lax.psum_scatter(attn_parts[0].astype(jnp.float32).astype(jnp.bfloat16),...  22.4 us
    reshape x2, local copies, waits for them, and re-layouts, lag_products(): skewed = flat.reshape(groups, block_rows, span + 1)  16 us
    ppermute x4, starting transfers between devices, shifted(): return lax.ppermute(x, axis, pairs)  12.2 us
    all_to_all x1, waiting for transfers between devices, shards(): lax.all_to_all(jnp.where(send_live[:, None, None], pieces[send_slot], 0),...  12.1 us
    reshape x2, local copies, waits for them, and re-layouts, lag_products(): cross.reshape(groups, block_rows * span)  10.4 us
    pad x2, local copies, waits for them, and re-layouts, lag_products(): jnp.pad(cross.reshape(groups, block_rows * span), ((0, 0), (0, block_rows)))  7.74 us
  transfers between devices with their start and end apart: 6, of which 3 were waited for; matrix products, arithmetic and copies ran while one was open for 23% of the time, Pallas kernels for 0%

commit v1 on v0

v1 whole, which is shorter than its diff:
```python
import functools
import math

import jax
import jax.numpy as jnp
from jax import lax
from jax.experimental import pallas as pl
from jax.experimental.pallas import tpu as pltpu
from jax.sharding import PartitionSpec as P

GROUP = 16
LANES = 256
PARAMS = pltpu.CompilerParams(vmem_limit_bytes=32 * 1024 * 1024)


def shifted(x, axis, by):
    size = lax.axis_size(axis)
    pairs = [(i, i + by) for i in range(size) if 0 <= i + by < size]
    return lax.ppermute(x, axis, pairs)


def cost(flops, bytes_accessed):
    return pl.CostEstimate(flops=flops, bytes_accessed=bytes_accessed, transcendentals=0)


def call(body, grid, in_specs, out_specs, out_shape, flops, moved, scratch=()):
    return pl.pallas_call(
        body,
        grid=grid,
        in_specs=in_specs,
        out_specs=out_specs,
        out_shape=out_shape,
        scratch_shapes=list(scratch),
        compiler_params=PARAMS,
        cost_estimate=cost(flops, moved),
    )


def streams_kernel(feat_ref, rim_ref, wt_ref, streams_ref, kv_ref, ext):
    rows = feat_ref.shape[1]
    taps = wt_ref.shape[1]
    found = []
    for s in range(3):
        ext[8 - taps + 1 : 8] = rim_ref[s].astype(jnp.float32)
        ext[8:] = feat_ref[s].astype(jnp.float32)
        total = wt_ref[s, 0:1, :] * ext[8:]
        for lag in range(1, taps):
            total = total + wt_ref[s, lag : lag + 1, :] * ext[8 - lag : 8 - lag + rows]
        streams_ref[s] = total
        found.append(total)
    kv_ref[...] = (found[1] * found[2]).astype(kv_ref.dtype)


def plane(rows, axis):
    return lax.broadcasted_iota(jnp.int32, (rows, rows), axis)


def mixed_kernel(filt_ref, before_ref, own_ref, mixed_ref):
    taps = filt_ref.shape[1]
    width = own_ref.shape[1]
    window = jnp.concatenate([before_ref[...], own_ref[...]], axis=0)
    t, s = plane(taps, 0), plane(taps, 1)
    owner = lax.broadcasted_iota(jnp.int32, (taps, width), 1) // GROUP
    total = jnp.zeros((taps, width), jnp.float32)
    for g in range(width // GROUP):
        line = jnp.broadcast_to(filt_ref[g : g + 1, :], (taps, taps))
        wheel = pltpu.roll(line, 0, 1, stride=1, stride_axis=0)
        table = jnp.concatenate(
            [jnp.where(s > t, wheel, 0.0), jnp.where(s <= t, wheel, 0.0)], axis=1
        ).astype(own_ref.dtype)
        product = jnp.dot(table, window, preferred_element_type=jnp.float32)
        total = jnp.where(owner == g, product, total)
    mixed_ref[...] = total


def back_kernel(
    filt_ref, dmix_ref, after_ref, kv_ref, before_ref, streams_ref, dq_ref, feat_ref, rim_ref,
    dstreams_ref, med_ref, short_ref, ext,
):
    taps = filt_ref.shape[1]
    width = dmix_ref.shape[1]
    kind = dmix_ref.dtype
    t, s = plane(taps, 0), plane(taps, 1)
    owner = lax.broadcasted_iota(jnp.int32, (taps, width), 1) // GROUP
    dmix = dmix_ref[...]
    window = jnp.concatenate([dmix, after_ref[...]], axis=0)
    flip = jnp.where(t + s == taps - 1, 1.0, 0.0).astype(kind)
    flipped = jnp.dot(flip, dmix, preferred_element_type=jnp.float32)
    keyval = jnp.concatenate([before_ref[...], kv_ref[...]], axis=0)
    total = jnp.zeros((taps, width), jnp.float32)
    for g in range(width // GROUP):
        line = jnp.broadcast_to(filt_ref[g : g + 1, :], (taps, taps))
        wheel = pltpu.roll(line, 0, 1, stride=1, stride_axis=0)
        table = jnp.concatenate(
            [jnp.where(s >= t, wheel, 0.0), jnp.where(s < t, wheel, 0.0)], axis=1
        ).astype(kind)
        product = jnp.dot(table, window, preferred_element_type=jnp.float32)
        total = jnp.where(owner == g, product, total)
        left = jnp.where(owner == g, flipped, 0.0).astype(kind)
        cross = lax.dot_general(
            left, keyval, (((1,), (1,)), ((), ())), preferred_element_type=jnp.float32
        )
        ring = jnp.where(s + t <= taps - 1, cross[:, taps:], cross[:, :taps])
        ring = pltpu.roll(ring, 0, 1, stride=1, stride_axis=0)
        med_ref[g : g + 1, :] = jnp.sum(ring, axis=0, keepdims=True)
    rows = feat_ref.shape[1]
    short_taps = short_ref.shape[1]
    parts = (dq_ref[...], total * streams_ref[1], total * streams_ref[0])
    for k in range(3):
        dstreams_ref[k] = parts[k]
        ext[8 - short_taps + 1 : 8] = rim_ref[k].astype(jnp.float32)
        ext[8:] = feat_ref[k].astype(jnp.float32)
        for lag in range(short_taps):
            short_ref[k, lag : lag + 1, :] = jnp.sum(
                parts[k] * ext[8 - lag : 8 - lag + rows], axis=0, keepdims=True
            )


def feat_kernel(ds_ref, rim_ref, wt_ref, out_ref, ext):
    rows = ds_ref.shape[1]
    taps = wt_ref.shape[1]
    for s in range(3):
        ext[0:rows] = ds_ref[s]
        ext[rows : rows + taps - 1] = rim_ref[s].astype(jnp.float32)
        total = wt_ref[s, 0:1, :] * ds_ref[s]
        for lag in range(1, taps):
            total = total + wt_ref[s, lag : lag + 1, :] * ext[lag : lag + rows]
        out_ref[s] = total.astype(out_ref.dtype)


def shards(features, out_grad, attn_parts, short_filt, med_filt, piece_home, piece_start):
    rows, width = out_grad.shape
    groups, taps = med_filt.shape
    short_taps = short_filt.shape[2]
    ctx_count = lax.axis_size("ctx")
    own_index = lax.axis_index("ctx")
    per_device = ctx_count // 2
    piece_rows = rows // per_device
    factor = 1.0 / math.sqrt(rows * ctx_count * GROUP)
    chunk = LANES if width % LANES == 0 else width
    steps = width // chunk
    grid = (steps,)
    near = chunk // GROUP

    def lead3(n):
        return pl.BlockSpec((3, n, chunk), lambda i: (0, 0, i))

    def flat(n):
        return pl.BlockSpec((n, chunk), lambda i: (0, i))

    filt_spec = pl.BlockSpec((near, taps), lambda i: (i, 0))
    f32, half = jnp.float32, features.dtype

    everyone = piece_home.reshape(ctx_count, per_device)
    positions = (piece_start // piece_rows).reshape(ctx_count, per_device)
    local_home = lax.dynamic_slice_in_dim(everyone, own_index, 1, 0)[0]
    device_ids = jnp.arange(ctx_count, dtype=jnp.int32)
    slot_ids = jnp.arange(per_device, dtype=jnp.int32)
    matches = local_home[None, :] == device_ids[:, None]
    send_slot = jnp.sum(jnp.where(matches, slot_ids[None, :], 0), axis=1)
    keyed = jnp.where(everyone == own_index, positions, -1)
    hits = jnp.any(keyed[:, :, None] == slot_ids[None, None, :], axis=1)
    source_of = jnp.sum(jnp.where(hits, device_ids[:, None], 0), axis=0)
    summed = lax.psum_scatter(attn_parts[0], "tp", scatter_dimension=1, tiled=True)
    pieces = summed.reshape(per_device, piece_rows, -1)
    attn_home = lax.all_to_all(
        pieces[send_slot], "ctx", split_axis=0, concat_axis=0, tiled=True
    )[source_of].reshape(rows, -1)

    short_weights = jnp.transpose(jnp.repeat(short_filt, GROUP, axis=1), (0, 2, 1)).astype(f32)
    filt = med_filt.astype(f32)
    filt_back = jnp.roll(filt[:, ::-1], 1, axis=1)
    stream_rim = shifted(features[:, rows - short_taps + 1 :, :], "ctx", 1)
    streams, keyval = call(
        streams_kernel,
        grid,
        [lead3(rows), lead3(short_taps - 1), lead3(short_taps)],
        (lead3(rows), flat(rows)),
        (
            jax.ShapeDtypeStruct((3, rows, width), f32),
            jax.ShapeDtypeStruct((rows, width), half),
        ),
        3 * 14 * rows * width,
        20 * rows * width,
        [pltpu.VMEM((rows + 8, chunk), f32)],
    )(features, stream_rim, short_weights)
    key_rim = shifted(keyval, "ctx", 1)
    mixed = call(
        mixed_kernel,
        grid,
        [filt_spec, flat(rows), flat(rows)],
        flat(rows),
        jax.ShapeDtypeStruct((rows, width), f32),
        4 * groups * taps * taps * chunk,
        8 * rows * width,
    )(filt_back, key_rim, keyval)

    grad = out_grad.astype(f32) + attn_home.astype(f32)
    dmix = (grad * streams[0]).astype(half)
    dquery = grad * mixed
    grad_rim = shifted(dmix, "ctx", -1)
    pair = streams[1:]
    dstreams, med_part, short_cols = call(
        back_kernel,
        grid,
        [
            filt_spec, flat(rows), flat(rows), flat(rows), flat(rows),
            pl.BlockSpec((2, rows, chunk), lambda i: (0, 0, i)),
            flat(rows), lead3(rows), lead3(short_taps - 1),
        ],
        (lead3(rows), filt_spec, lead3(short_taps)),
        (
            jax.ShapeDtypeStruct((3, rows, width), f32),
            jax.ShapeDtypeStruct((groups, taps), f32),
            jax.ShapeDtypeStruct((3, short_taps, width), f32),
        ),
        8 * groups * taps * taps * chunk,
        40 * rows * width,
        [pltpu.VMEM((rows + 8, chunk), f32)],
    )(filt, dmix, grad_rim, keyval, key_rim, pair, dquery, features, stream_rim)
    tail_rim = shifted(dstreams[:, : short_taps - 1].astype(half), "ctx", -1)
    feat_grad = call(
        feat_kernel,
        grid,
        [lead3(rows), lead3(short_taps - 1), lead3(short_taps)],
        lead3(rows),
        jax.ShapeDtypeStruct((3, rows, width), half),
        3 * 14 * rows * width,
        20 * rows * width,
        [pltpu.VMEM((rows + 8, chunk), f32)],
    )(dstreams, tail_rim, short_weights)
    member = (
        jnp.arange(width, dtype=jnp.int32)[:, None] // GROUP
        == jnp.arange(groups, dtype=jnp.int32)[None, :]
    ).astype(f32)
    short_part = jnp.einsum(
        "slw,wg->sgl", short_cols, member, precision=lax.Precision.HIGHEST
    )
    totals = lax.psum((short_part, med_part), "ctx")
    return (feat_grad, totals[0] * factor, totals[1][:, ::-1] * factor)


def solution(mesh):
    return jax.shard_map(
        shards,
        mesh=mesh,
        in_specs=(
            P(None, "ctx", "tp"),
            P("ctx", "tp"),
            P("tp", "ctx", None),
            P(None, "tp", None),
            P("tp", None),
            P(),
            P(),
        ),
        out_specs=(P(None, "ctx", "tp"), P(None, "tp", None), P("tp", None)),
        check_vma=False,
    )
```

time: 223 us -> 138 us (0.62)
  local copies, waits for them, and re-layouts: 87.8 us -> 7.46 us
  Pallas kernels: 0 us -> 14.1 us
  matrix products: 12.2 us -> 0.19 us
  other arithmetic: 14.9 us -> 3.99 us
  blocking collectives: 35.6 us -> 38.6 us
  waiting for transfers between devices: 39.3 us -> 41.9 us
    reshape x15 -> x0, local copies, waits for them, and re-layouts: 60 us -> none  [the longest x2 31.7 us: band_table(): return tiled.reshape(filt.shape[0], taps, 2 * taps - 1)]
    ppermute x4, waiting for transfers between devices: 4.08 us -> 18.4 us  [shifted(): return lax.ppermute(x, axis, pairs)]
    pallas_call x0 -> x4, Pallas kernels: none -> 14.1 us  [the longest x1 7.37 us: shards(): call(back_kernel, grid, [filt_spec, flat(rows), flat(rows), flat(rows), f...]
    all_to_all x1, waiting for transfers between devices: 12.1 us -> 0.01 us  [shards(): lax.all_to_all(pieces[send_slot], 'ctx', split_axis=0, concat_axis=0, til...]
    dot_general x4 -> x1, matrix products: 12.2 us -> 0.19 us  [shards(): jnp.einsum('slw,wg->sgl', short_cols, member, precision=lax.Precision.HIG...]
    pad x2 -> x0, local copies, waits for them, and re-layouts: 7.74 us -> none  [lag_products(): jnp.pad(cross.reshape(groups, block_rows * span), ((0, 0), (0, block_rows)))]
    unnamed x35 -> x8, local copies, waits for them, and re-layouts: 7.45 us -> 0.02 us
    reduce_sum x10 -> x0, other arithmetic: 6.11 us -> none  [the longest x2 3.73 us: lag_products(): total = total + jnp.sum(skewed[:, :, :taps], axis=1)]
  transfers between devices with their start and end apart: 6 -> 6, of which waited for: 3 -> 4; matrix products, arithmetic and copies ran while one was open for 23% -> 5% of each run, Pallas kernels for 0% -> 3%
where the time goes in v1:
time: 138 us
  waiting for transfers between devices  41.9 us (30%)
  blocking collectives  38.6 us (28%)
  starting transfers between devices  17.1 us (12%)
  between operations  14.2 us (10%)
  Pallas kernels  14.1 us (10%)
  local copies, waits for them, and re-layouts  7.46 us (5%)
  other arithmetic  3.99 us (3%)
    psum x1, blocking collectives, shards(): totals = lax.psum((short_part, med_part), 'ctx')  38.6 us
    reduce_scatter x1, waiting for transfers between devices, shards(): lax.psum_scatter(attn_parts[0], 'tp', scatter_dimension=1, tiled=True)  22.8 us
    ppermute x4, waiting for transfers between devices, shifted(): return lax.ppermute(x, axis, pairs)  18.4 us
    ppermute x4, starting transfers between devices, shifted(): return lax.ppermute(x, axis, pairs)  11.4 us
    pallas_call x1, Pallas kernels, shards(): call(back_kernel, grid, [filt_spec, flat(rows), flat(rows), flat(rows), f...  7.37 us
    all_to_all x1, starting transfers between devices, shards(): lax.all_to_all(pieces[send_slot], 'ctx', split_axis=0, concat_axis=0, til...  5.65 us
  transfers between devices with their start and end apart: 6, of which 4 were waited for; matrix products, arithmetic and copies ran while one was open for 5% of the time, Pallas kernels for 3%

profile of v1, /device:TPU:0, one launch (start us, length us, event | category | flops | bytes accessed | tf_op | source)
XLA Modules:
  0.0 137.6 jit_solution(1720400691441640076)
XLA Ops:
  7.2 0.0 reduce-scatter.2.cloned.1.call-start
  7.2 0.0 copy-start.3
  7.2 0.7 reduce-scatter.2.cloned.1.call-update
  7.9 0.8 slice.25
  8.7 4.9 %collective-permute-start = (bf16[3,6,1024]{2,1,0:T(8,128)(2,1)S(1)}, bf16[3,6,1024]{2,1,0:T(8,128)(2,1)S(1)}, u32[]{:S(2)}, u32[]{:S(2)}) collective-permute-start(bf16[3,6,1024]{2,1,0:T(8,128)(2,1)S(1)} %slice.25), channel_id=1, source_target_pairs={{0,4},{4,8},{8,12},{12,16},{16,20},{20,24},{24,28},{1,5},{5,9},{9,... | collective-permute-start | bytes 110600 | tf_op jit(solution)/shard_map/ppermute | solution.py:19
  13.6 0.7 reshape.94
  14.4 0.7 and_select_fusion
  15.0 0.1 reshape.95
  15.1 0.1 select_reduce_fusion.1
  15.2 22.8 %reduce-scatter.2.cloned.1.call-done = bf16[128,1024]{1,0:T(8,128)(2,1)} async-done(((bf16[128,4096]{1,0:T(8,128)(2,1)}), bf16[128,1024]{1,0:T(8,128)(2,1)}) %reduce-scatter.2.cloned.1.call-update) | async-done | bytes 262160 | tf_op jit(solution)/shard_map/reduce_scatter | solution.py:164
  38.0 0.0 copy-start
  38.0 2.4 %gather_fusion = bf16[8,32,1024]{2,1,0:T(8,128)(2,1)} fusion(bf16[4,32,1024]{2,1,0:T(8,128)(2,1)} %bitcast.34, s32[1024]{0:T(1024)S(1)} %pad_clamp_fusion.1), kind=kCustom, calls=%fused_computation | custom fusion | bytes 1048608 | tf_op jit(solution)/shard_map/gather | solution.py:167
  40.4 0.0 copy-start.1
  40.4 5.6 %all-to-all-start = ((bf16[8,32,1024]{2,1,0:T(8,128)(2,1)}), bf16[8,32,1024]{2,1,0:T(8,128)(2,1)}, u32[]{:S(2)}, u32[]{:S(2)}) async-start(bf16[8,32,1024]{2,1,0:T(8,128)(2,1)} %gather_fusion), calls=%async_computation.1 | async-start | bytes 1048576 | tf_op jit(solution)/shard_map/all_to_all | solution.py:166
  46.1 0.1 copy.10
  46.2 0.1 select_reduce_fusion
  46.3 0.0 copy-done.3
  46.3 0.2 broadcast_in_dim.39
  46.6 0.4 convert_element_type.29
  46.9 0.0 collective-permute-done.rim_ref
  46.9 0.0 copy-done
  46.9 1.9 %shard_map.94 = (f32[3,128,1024]{2,1,0:T(8,128)S(1)}, bf16[128,1024]{1,0:T(8,128)(2,1)S(1)}) custom-call(bf16[3,128,1024]{2,1,0:T(8,128)(2,1)S(1)} %copy-done, bf16[3,6,1024]{2,1,0:T(8,128)(2,1)S(1)} %collective-permute-done.rim_ref, f32[3,7,1024]{2,1,0:T(8,128)S(1)} %bitcast.31), custom_call_target="tpu_custom_call" | custom-call | flops 5505024 | bytes 2621440 | tf_op jit(solution)/shard_map/pallas_call | solution.py:174
  48.9 3.9 %collective-permute-start.2 = (bf16[128,1024]{1,0:T(8,128)(2,1)S(1)}, bf16[128,1024]{1,0:T(8,128)(2,1)S(1)}, u32[]{:S(2)}, u32[]{:S(2)}) collective-permute-start(bf16[128,1024]{1,0:T(8,128)(2,1)S(1)} %get-tuple-element.9.own_ref.kv_ref), channel_id=1, source_target_pairs={{0,4},{4,8},{8,12},{12,16},{16,20},{20,24},{24,28},{1,5},{5,9},{9,... | collective-permute-start | bytes 786440 | tf_op jit(solution)/shard_map/ppermute | solution.py:19
  52.9 0.0 copy-done.1
  52.9 0.1 slice.37
  52.9 0.1 slice.30
  53.0 0.6 pad_clamp_fusion
  53.6 0.1 pad_maximum_fusion.filt_ref
  53.7 5.4 %collective-permute-done.2.before_ref = bf16[128,1024]{1,0:T(8,128)(2,1)S(1)} collective-permute-done((bf16[128,1024]{1,0:T(8,128)(2,1)S(1)}, bf16[128,1024]{1,0:T(8,128)(2,1)S(1)}, u32[]{:S(2)}, u32[]{:S(2)}) %collective-permute-start.2) | collective-permute-done | bytes 262176 | tf_op jit(solution)/shard_map/ppermute | solution.py:19
  59.1 2.1 %shard_map.95 = f32[128,1024]{1,0:T(8,128)S(1)} custom-call(f32[64,128]{1,0:T(8,128)S(1)} %pad_maximum_fusion.filt_ref, bf16[128,1024]{1,0:T(8,128)(2,1)S(1)} %collective-permute-done.2.before_ref, bf16[128,1024]{1,0:T(8,128)(2,1)S(1)} %get-tuple-element.9.own_ref.kv_ref), custom_call_target="tpu_custom_call" | custom-call | flops 1073741824 | bytes 1048576 | tf_op jit(solution)/shard_map/pallas_call | solution.py:188
  61.2 0.0 all-to-all-done
  61.3 2.4 %gather_fusion.1 = bf16[4,32,1024]{2,1,0:T(8,128)(2,1)} fusion(bf16[8,32,1024]{2,1,0:T(8,128)(2,1)} %all-to-all-done, s32[1024]{0:T(1024)} %pad_clamp_fusion), kind=kCustom, calls=%fused_computation.1 | custom fusion | bytes 524304 | tf_op jit(solution)/shard_map/gather | solution.py:166
  63.7 0.0 copy-start.2
  63.7 1.2 fusion.1
  64.9 1.3 collective-permute-start.1
  66.2 0.0 copy-done.2
  66.2 0.1 slice.27.streams_ref
  66.3 9.0 %collective-permute-done.1.after_ref = bf16[128,1024]{1,0:T(8,128)(2,1)S(1)} collective-permute-done((bf16[128,1024]{1,0:T(8,128)(2,1)S(1)}, bf16[128,1024]{1,0:T(8,128)(2,1)S(1)}, u32[]{:S(2)}, u32[]{:S(2)}) %collective-permute-start.1) | collective-permute-done | bytes 262176 | tf_op jit(solution)/shard_map/ppermute | solution.py:19
  75.2 7.4 %shard_map.96 = (f32[3,128,1024]{2,1,0:T(8,128)S(1)}, f32[64,128]{1,0:T(8,128)S(1)}, f32[3,7,1024]{2,1,0:T(8,128)S(1)}) custom-call(f32[64,128]{1,0:T(8,128)S(1)} %convert_element_type.24.filt_ref, bf16[128,1024]{1,0:T(8,128)(2,1)S(1)} %get-tuple-element.16.dmix_ref, bf16[128,1024]{1,0:T(8,128)(2,1)S(1)} %collective-permute-done.1.after_ref, ...), custom_call_target="tpu_custom_call" | custom-call | flops 2147483648 | bytes 5242880 | tf_op jit(solution)/shard_map/pallas_call | solution.py:203
  82.6 0.1 rev.4
  82.7 0.2 convolution_bitcast_fusion
  82.9 38.6 %all-reduce = (f32[3,64,7]{1,2,0:T(8,128)S(1)}, f32[64,128]{1,0:T(8,128)S(1)}) all-reduce(f32[3,64,7]{1,2,0:T(8,128)S(1)} %convolution_bitcast_fusion, f32[64,128]{1,0:T(8,128)S(1)} %rev.4), channel_id=1, replica_groups=mesh['ctx'=8,'tp'=4] {'ctx'}, use_global_device_ids=true, to_apply=%region_4.5 | all-reduce | flops 9536 | bytes 76288 | tf_op jit(solution)/shard_map/psum | solution.py:239
  121.5 0.6 broadcast_multiply_fusion
  122.1 1.3 collective-permute-start.3
  123.4 0.6 broadcast_multiply_fusion.1
  124.0 4.1 %collective-permute-done.3.rim_ref = bf16[3,6,1024]{2,1,0:T(8,128)(2,1)S(1)} collective-permute-done((bf16[3,6,1024]{2,1,0:T(8,128)(2,1)S(1)}, bf16[3,6,1024]{2,1,0:T(8,128)(2,1)S(1)}, u32[]{:S(2)}, u32[]{:S(2)}) %collective-permute-start.3) | collective-permute-done | bytes 36896 | tf_op jit(solution)/shard_map/ppermute | solution.py:19
  128.1 2.6 %shard_map.97 = bf16[3,128,1024]{2,1,0:T(8,128)(2,1)} custom-call(f32[3,128,1024]{2,1,0:T(8,128)S(1)} %get-tuple-element.10.ds_ref, bf16[3,6,1024]{2,1,0:T(8,128)(2,1)S(1)} %collective-permute-done.3.rim_ref, f32[3,7,1024]{2,1,0:T(8,128)S(1)} %bitcast.32), custom_call_target="tpu_custom_call" | custom-call | flops 5505024 | bytes 2621440 | tf_op jit(solution)/shard_map/pallas_call | solution.py:222
  (10 shorter events, 0.1 us)
Async XLA Ops:
  7.2 30.9 %reduce-scatter.2.cloned.1.call-start = ((), (), s32[]{:S(2)}) async-start(), calls=%async_computation.2 | async-start | bytes 1310720 | tf_op jit(solution)/shard_map/reduce_scatter | solution.py:164
  7.2 39.1 %copy-start.3 = (bf16[3,64,7]{1,2,0:T(8,128)(2,1)S(1)}, bf16[3,64,7]{1,2,0:T(8,128)(2,1)}, u32[]{:S(2)}) copy-start(bf16[3,64,7]{1,2,0:T(8,128)(2,1)} %param.10) | copy-start | bytes 8068
  8.7 38.2 %collective-permute-start = (bf16[3,6,1024]{2,1,0:T(8,128)(2,1)S(1)}, bf16[3,6,1024]{2,1,0:T(8,128)(2,1)S(1)}, u32[]{:S(2)}, u32[]{:S(2)}) collective-permute-start(bf16[3,6,1024]{2,1,0:T(8,128)(2,1)S(1)} %slice.25), channel_id=1, source_target_pairs={{0,4},{4,8},{8,12},{12,16},{16,20},{20,24},{24,28},{1,5},{5,9},{9,... | collective-permute-start | bytes 110600 | tf_op jit(solution)/shard_map/ppermute | solution.py:19
  38.0 8.9 %copy-start = (bf16[3,128,1024]{2,1,0:T(8,128)(2,1)S(1)}, bf16[3,128,1024]{2,1,0:T(8,128)(2,1)}, u32[]{:S(2)}) copy-start(bf16[3,128,1024]{2,1,0:T(8,128)(2,1)} %feat_ref.3) | copy-start | bytes 2359300
  40.4 12.4 %copy-start.1 = (bf16[64,128]{1,0:T(8,128)(2,1)S(1)}, bf16[64,128]{1,0:T(8,128)(2,1)}, u32[]{:S(2)}) copy-start(bf16[64,128]{1,0:T(8,128)(2,1)} %param.11) | copy-start | bytes 49156
  40.4 20.8 %all-to-all-start = ((bf16[8,32,1024]{2,1,0:T(8,128)(2,1)}), bf16[8,32,1024]{2,1,0:T(8,128)(2,1)}, u32[]{:S(2)}, u32[]{:S(2)}) async-start(bf16[8,32,1024]{2,1,0:T(8,128)(2,1)} %gather_fusion), calls=%async_computation.1 | async-start | bytes 1048576 | tf_op jit(solution)/shard_map/all_to_all | solution.py:166
  48.9 10.2 %collective-permute-start.2 = (bf16[128,1024]{1,0:T(8,128)(2,1)S(1)}, bf16[128,1024]{1,0:T(8,128)(2,1)S(1)}, u32[]{:S(2)}, u32[]{:S(2)}) collective-permute-start(bf16[128,1024]{1,0:T(8,128)(2,1)S(1)} %get-tuple-element.9.own_ref.kv_ref), channel_id=1, source_target_pairs={{0,4},{4,8},{8,12},{12,16},{16,20},{20,24},{24,28},{1,5},{5,9},{9,... | collective-permute-start | bytes 786440 | tf_op jit(solution)/shard_map/ppermute | solution.py:19
  63.7 2.5 %copy-start.2 = (bf16[64,128]{1,0:T(8,128)(2,1)S(1)}, bf16[64,128]{1,0:T(8,128)(2,1)}, u32[]{:S(2)}) copy-start(bf16[64,128]{1,0:T(8,128)(2,1)} %param.11) | copy-start | bytes 49156
  64.9 10.4 %collective-permute-start.1 = (bf16[128,1024]{1,0:T(8,128)(2,1)S(1)}, bf16[128,1024]{1,0:T(8,128)(2,1)S(1)}, u32[]{:S(2)}, u32[]{:S(2)}) collective-permute-start(bf16[128,1024]{1,0:T(8,128)(2,1)S(1)} %get-tuple-element.16.dmix_ref), channel_id=1, source_target_pairs={{4,0},{8,4},{12,8},{16,12},{20,16},{24,20},{28,24},{5,1},{9,5},{13... | collective-permute-start | bytes 786440 | tf_op jit(solution)/shard_map/ppermute | solution.py:19
  122.1 6.0 %collective-permute-start.3 = (bf16[3,6,1024]{2,1,0:T(8,128)(2,1)S(1)}, bf16[3,6,1024]{2,1,0:T(8,128)(2,1)S(1)}, u32[]{:S(2)}, u32[]{:S(2)}) collective-permute-start(bf16[3,6,1024]{2,1,0:T(8,128)(2,1)S(1)} %slice.41), channel_id=1, source_target_pairs={{4,0},{8,4},{12,8},{16,12},{20,16},{24,20},{28,24},{5,1},{9,5},{13... | collective-permute-start | bytes 110600 | tf_op jit(solution)/shard_map/ppermute | solution.py:19
Sparse Core Ops, SparseCore 0:
  10.5 27.4 reduce-scatter.1

commit v2 on v1

--- a/solution.py
+++ b/solution.py
@@ -9,6 +9,7 @@
 from jax.sharding import PartitionSpec as P
 
 GROUP = 16
+MESH = pl.DeviceIdType.MESH
 LANES = 256
 PARAMS = pltpu.CompilerParams(vmem_limit_bytes=32 * 1024 * 1024)
 
@@ -75,7 +76,7 @@
 
 def back_kernel(
     filt_ref, dmix_ref, after_ref, kv_ref, before_ref, streams_ref, dq_ref, feat_ref, rim_ref,
-    dstreams_ref, med_ref, short_ref, ext,
+    dstreams_ref, med_ref, short_ref, head_ref, ext,
 ):
     taps = filt_ref.shape[1]
     width = dmix_ref.shape[1]
@@ -108,6 +109,7 @@
     parts = (dq_ref[...], total * streams_ref[1], total * streams_ref[0])
     for k in range(3):
         dstreams_ref[k] = parts[k]
+        head_ref[k] = parts[k][:8].astype(head_ref.dtype)
         ext[8 - short_taps + 1 : 8] = rim_ref[k].astype(jnp.float32)
         ext[8:] = feat_ref[k].astype(jnp.float32)
         for lag in range(short_taps):
@@ -116,16 +118,72 @@
             )
 
 
-def feat_kernel(ds_ref, rim_ref, wt_ref, out_ref, ext):
-    rows = ds_ref.shape[1]
+def final_kernel(
+    n, part_ref, ds_ref, head_ref, wt_ref, feat_ref, total_ref,
+    landed, gathered, rim, ext, send1, recv1, send2, recv2, send_rim, recv_rim,
+):
+    me = lax.axis_index("ctx")
+    rows, width = ds_ref.shape[1:]
     taps = wt_ref.shape[1]
+    chunk = ext.shape[1]
+    barrier = pltpu.get_barrier_semaphore()
+
+    def greet(k, carry):
+        pl.semaphore_signal(
+            barrier, inc=1, device_id={"ctx": lax.rem(me + k, n)}, device_id_type=MESH
+        )
+        return carry
+
+    lax.fori_loop(1, n, greet, 0)
+    pl.semaphore_wait(barrier, n - 1)
+
+    def scatter(k):
+        peer = lax.rem(me + k, n)
+        return pltpu.make_async_remote_copy(
+            part_ref.at[peer], landed.at[k], send1.at[k], recv1.at[k],
+            device_id={"ctx": peer}, device_id_type=MESH,
+        )
+
+    def gather(k):
+        peer = lax.rem(me + k, n)
+        return pltpu.make_async_remote_copy(
+            gathered.at[me], gathered.at[me], send2.at[k], recv2.at[k],
+            device_id={"ctx": peer}, device_id_type=MESH,
+        )
+
+    def each(copy, act):
+        def step(k, carry):
+            act(copy(k))
+            return carry
+
+        lax.fori_loop(1, n, step, 0)
+
+    halo = pltpu.make_async_remote_copy(
+        head_ref, rim, send_rim, recv_rim,
+        device_id={"ctx": lax.rem(me + n - 1, n)}, device_id_type=MESH,
+    )
+    halo.start()
+    each(scatter, lambda c: c.start())
+    landed[0] = part_ref[me]
+    each(scatter, lambda c: c.wait())
+    total = landed[0]
+    for k in range(1, n):
+        total = total + landed[k]
+    gathered[me] = total
+    each(gather, lambda c: c.start())
+    halo.wait()
+    live = jnp.where(me == n - 1, 0.0, 1.0)
     for s in range(3):
-        ext[0:rows] = ds_ref[s]
-        ext[rows : rows + taps - 1] = rim_ref[s].astype(jnp.float32)
-        total = wt_ref[s, 0:1, :] * ds_ref[s]
-        for lag in range(1, taps):
-            total = total + wt_ref[s, lag : lag + 1, :] * ext[lag : lag + rows]
-        out_ref[s] = total.astype(out_ref.dtype)
+        for c in range(width // chunk):
+            cols = slice(c * chunk, (c + 1) * chunk)
+            ext[0:rows] = ds_ref[s, :, cols]
+            ext[rows : rows + 8] = live * rim[s, :, cols].astype(jnp.float32)
+            total = wt_ref[s, 0:1, cols] * ds_ref[s, :, cols]
+            for lag in range(1, taps):
+                total = total + wt_ref[s, lag : lag + 1, cols] * ext[lag : lag + rows]
+            feat_ref[s, :, cols] = total.astype(feat_ref.dtype)
+    each(gather, lambda c: c.wait())
+    total_ref[...] = gathered[...]
 
 
 def shards(features, out_grad, attn_parts, short_filt, med_filt, piece_home, piece_start):
@@ -200,7 +258,7 @@
     dquery = grad * mixed
     grad_rim = shifted(dmix, "ctx", -1)
     pair = streams[1:]
-    dstreams, med_part, short_cols = call(
+    dstreams, med_part, short_cols, heads = call(
         back_kernel,
         grid,
         [
@@ -208,36 +266,59 @@
             pl.BlockSpec((2, rows, chunk), lambda i: (0, 0, i)),
             flat(rows), lead3(rows), lead3(short_taps - 1),
         ],
-        (lead3(rows), filt_spec, lead3(short_taps)),
+        (lead3(rows), filt_spec, lead3(short_taps), lead3(8)),
         (
             jax.ShapeDtypeStruct((3, rows, width), f32),
             jax.ShapeDtypeStruct((groups, taps), f32),
             jax.ShapeDtypeStruct((3, short_taps, width), f32),
+            jax.ShapeDtypeStruct((3, 8, width), half),
         ),
         8 * groups * taps * taps * chunk,
         40 * rows * width,
         [pltpu.VMEM((rows + 8, chunk), f32)],
     )(filt, dmix, grad_rim, keyval, key_rim, pair, dquery, features, stream_rim)
-    tail_rim = shifted(dstreams[:, : short_taps - 1].astype(half), "ctx", -1)
-    feat_grad = call(
-        feat_kernel,
-        grid,
-        [lead3(rows), lead3(short_taps - 1), lead3(short_taps)],
-        lead3(rows),
-        jax.ShapeDtypeStruct((3, rows, width), half),
-        3 * 14 * rows * width,
-        20 * rows * width,
-        [pltpu.VMEM((rows + 8, chunk), f32)],
-    )(dstreams, tail_rim, short_weights)
     member = (
         jnp.arange(width, dtype=jnp.int32)[:, None] // GROUP
-        == jnp.arange(groups, dtype=jnp.int32)[None, :]
-    ).astype(f32)
-    short_part = jnp.einsum(
-        "slw,wg->sgl", short_cols, member, precision=lax.Precision.HIGHEST
-    )
-    totals = lax.psum((short_part, med_part), "ctx")
-    return (feat_grad, totals[0] * factor, totals[1][:, ::-1] * factor)
+        == jnp.arange(max(groups, taps), dtype=jnp.int32)[None, :]
+    ).astype(f32)[:, :taps]
+    short_part = jnp.dot(
+        short_cols.reshape(3 * short_taps, width), member, precision=lax.Precision.HIGHEST
+    )
+    used = groups + 3 * short_taps
+    share = -(-used // ctx_count)
+    parts = jnp.concatenate(
+        [med_part, short_part, jnp.zeros((share * ctx_count - used, taps), f32)], axis=0
+    ).reshape(ctx_count, share, taps)
+    vmem = pl.BlockSpec(memory_space=pltpu.VMEM)
+    dma = pltpu.SemaphoreType.DMA
+    feat_grad, totals = pl.pallas_call(
+        functools.partial(final_kernel, ctx_count),
+        in_specs=[vmem] * 4,
+        out_specs=(vmem, vmem),
+        out_shape=(
+            jax.ShapeDtypeStruct((3, rows, width), half),
+            jax.ShapeDtypeStruct(parts.shape, f32),
+        ),
+        scratch_shapes=[
+            pltpu.VMEM(parts.shape, f32),
+            pltpu.VMEM(parts.shape, f32),
+            pltpu.VMEM((3, 8, width), half),
+            pltpu.VMEM((rows + 8, chunk), f32),
+            dma((ctx_count,)), dma((ctx_count,)), dma((ctx_count,)), dma((ctx_count,)),
+            dma, dma,
+        ],
+        compiler_params=pltpu.CompilerParams(
+            collective_id=1, has_side_effects=True, vmem_limit_bytes=32 * 1024 * 1024
+        ),
+        cost_estimate=cost(3 * 14 * rows * width, 20 * rows * width),
+    )(parts, dstreams, heads, short_weights)
+    flat_totals = totals.reshape(-1, taps)
+    short_total = flat_totals[groups:used, :groups].reshape(3, short_taps, groups)
+    return (
+        feat_grad,
+        jnp.transpose(short_total, (0, 2, 1)) * factor,
+        flat_totals[:groups, ::-1] * factor,
+    )
 
 
 def solution(mesh):

time: 138 us -> 110 us (0.80)
  blocking collectives: 38.6 us -> 0 us
  Pallas kernels: 14.1 us -> 28.7 us
  waiting for transfers between devices: 41.9 us -> 37.8 us
  local copies, waits for them, and re-layouts: 7.46 us -> 9.04 us
    psum x1 -> x0, blocking collectives: 38.6 us -> none  [shards(): totals = lax.psum((short_part, med_part), 'ctx')]
    pallas_call x1, Pallas kernels: 2.65 us -> 17.2 us  [shards(): pl.pallas_call(functools.partial(final_kernel, ctx_count), in_specs=[vmem...]
    ppermute x4 -> x3, waiting for transfers between devices: 18.4 us -> 14.3 us  [shifted(): return lax.ppermute(x, axis, pairs)]
    ppermute x4 -> x3, starting transfers between devices: 11.4 us -> 10.1 us  [shifted(): return lax.ppermute(x, axis, pairs)]
  transfers between devices with their start and end apart: 6 -> 5, of which waited for: 4 -> 3; matrix products, arithmetic and copies ran while one was open for 5% -> 6% of each run, Pallas kernels for 3% -> 4%
where the time goes in v2:
time: 110 us; the launch traced here: 109 us
  waiting for transfers between devices  37.8 us (34%)
  Pallas kernels  28.7 us (26%)
  starting transfers between devices  15.8 us (14%)
  between operations  14.2 us (13%)
  local copies, waits for them, and re-layouts  9.04 us (8%)
  other arithmetic  3.48 us (3%)
    reduce_scatter x1, waiting for transfers between devices, shards(): lax.psum_scatter(attn_parts[0], 'tp', scatter_dimension=1, tiled=True)  22.8 us
    pallas_call x1, Pallas kernels, shards(): pl.pallas_call(functools.partial(final_kernel, ctx_count), in_specs=[vmem...  17.2 us
    ppermute x3, waiting for transfers between devices, shifted(): return lax.ppermute(x, axis, pairs)  14.3 us
    ppermute x3, starting transfers between devices, shifted(): return lax.ppermute(x, axis, pairs)  10.1 us
    pallas_call x1, Pallas kernels, shards(): call(back_kernel, grid, [filt_spec, flat(rows), flat(rows), flat(rows), f...  7.4 us
    all_to_all x1, starting transfers between devices, shards(): lax.all_to_all(pieces[send_slot], 'ctx', split_axis=0, concat_axis=0, til...  5.65 us
    gather x1, local copies, waits for them, and re-layouts, shards(): lax.all_to_all(pieces[send_slot], 'ctx', split_axis=0, concat_axis=0, til...  2.43 us
    gather x1, local copies, waits for them, and re-layouts, shards(): pieces[send_slot]  2.39 us
  transfers between devices with their start and end apart: 5, of which 3 were waited for; matrix products, arithmetic and copies ran while one was open for 6% of the time, Pallas kernels for 4%

profile of v2, /device:TPU:0, one launch (start us, length us, event | category | flops | bytes accessed | tf_op | source)
XLA Modules:
  0.0 109.5 jit_solution(16614261105203426132)
XLA Ops:
  7.2 0.0 reduce-scatter.2.cloned.1.call-start
  7.2 0.0 copy-start.3
  7.2 0.7 reduce-scatter.2.cloned.1.call-update
  7.9 0.8 slice.27
  8.7 4.9 %collective-permute-start = (bf16[3,6,1024]{2,1,0:T(8,128)(2,1)S(1)}, bf16[3,6,1024]{2,1,0:T(8,128)(2,1)S(1)}, u32[]{:S(2)}, u32[]{:S(2)}) collective-permute-start(bf16[3,6,1024]{2,1,0:T(8,128)(2,1)S(1)} %slice.27), channel_id=1, source_target_pairs={{0,4},{4,8},{8,12},{12,16},{16,20},{20,24},{24,28},{1,5},{5,9},{9,... | collective-permute-start | bytes 110600 | tf_op jit(solution)/shard_map/ppermute | solution.py:20
  13.6 0.7 reshape.106
  14.4 0.7 and_select_fusion
  15.0 0.1 reshape.107
  15.1 0.1 select_reduce_fusion.1
  15.2 22.8 %reduce-scatter.2.cloned.1.call-done = bf16[128,1024]{1,0:T(8,128)(2,1)} async-done(((bf16[128,4096]{1,0:T(8,128)(2,1)}), bf16[128,1024]{1,0:T(8,128)(2,1)}) %reduce-scatter.2.cloned.1.call-update) | async-done | bytes 262160 | tf_op jit(solution)/shard_map/reduce_scatter | solution.py:222
  38.0 0.0 copy-start
  38.0 2.4 %gather_fusion = bf16[8,32,1024]{2,1,0:T(8,128)(2,1)} fusion(bf16[4,32,1024]{2,1,0:T(8,128)(2,1)} %bitcast.30, s32[1024]{0:T(1024)S(1)} %pad_clamp_fusion.1), kind=kCustom, calls=%fused_computation | custom fusion | bytes 1048608 | tf_op jit(solution)/shard_map/gather | solution.py:225
  40.4 0.0 copy-start.1
  40.4 5.6 %all-to-all-start = ((bf16[8,32,1024]{2,1,0:T(8,128)(2,1)}), bf16[8,32,1024]{2,1,0:T(8,128)(2,1)}, u32[]{:S(2)}, u32[]{:S(2)}) async-start(bf16[8,32,1024]{2,1,0:T(8,128)(2,1)} %gather_fusion), calls=%async_computation.1 | async-start | bytes 1048576 | tf_op jit(solution)/shard_map/all_to_all | solution.py:224
  46.1 0.1 copy.10
  46.2 0.1 select_reduce_fusion
  46.3 0.0 copy-done.3
  46.3 0.2 broadcast_in_dim.42
  46.6 0.4 convert_element_type.28
  46.9 0.0 collective-permute-done.rim_ref
  46.9 0.0 copy-done
  46.9 1.9 %shard_map.94 = (f32[3,128,1024]{2,1,0:T(8,128)S(1)}, bf16[128,1024]{1,0:T(8,128)(2,1)S(1)}) custom-call(bf16[3,128,1024]{2,1,0:T(8,128)(2,1)S(1)} %copy-done, bf16[3,6,1024]{2,1,0:T(8,128)(2,1)S(1)} %collective-permute-done.rim_ref, f32[3,7,1024]{2,1,0:T(8,128)S(1)} %bitcast.27), custom_call_target="tpu_custom_call" | custom-call | flops 5505024 | bytes 2621440 | tf_op jit(solution)/shard_map/pallas_call | solution.py:232
  48.9 3.9 %collective-permute-start.2 = (bf16[128,1024]{1,0:T(8,128)(2,1)S(1)}, bf16[128,1024]{1,0:T(8,128)(2,1)S(1)}, u32[]{:S(2)}, u32[]{:S(2)}) collective-permute-start(bf16[128,1024]{1,0:T(8,128)(2,1)S(1)} %get-tuple-element.12.own_ref.kv_ref), channel_id=1, source_target_pairs={{0,4},{4,8},{8,12},{12,16},{16,20},{20,24},{24,28},{1,5},{5,9},{9,... | collective-permute-start | bytes 786440 | tf_op jit(solution)/shard_map/ppermute | solution.py:20
  52.9 0.0 copy-done.1
  52.9 0.1 slice.40
  52.9 0.1 slice.32
  53.0 0.6 pad_clamp_fusion
  53.6 0.1 pad_maximum_fusion.filt_ref
  53.7 5.4 %collective-permute-done.2.before_ref = bf16[128,1024]{1,0:T(8,128)(2,1)S(1)} collective-permute-done((bf16[128,1024]{1,0:T(8,128)(2,1)S(1)}, bf16[128,1024]{1,0:T(8,128)(2,1)S(1)}, u32[]{:S(2)}, u32[]{:S(2)}) %collective-permute-start.2) | collective-permute-done | bytes 262176 | tf_op jit(solution)/shard_map/ppermute | solution.py:20
  59.1 2.1 %shard_map.95 = f32[128,1024]{1,0:T(8,128)S(1)} custom-call(f32[64,128]{1,0:T(8,128)S(1)} %pad_maximum_fusion.filt_ref, bf16[128,1024]{1,0:T(8,128)(2,1)S(1)} %collective-permute-done.2.before_ref, bf16[128,1024]{1,0:T(8,128)(2,1)S(1)} %get-tuple-element.12.own_ref.kv_ref), custom_call_target="tpu_custom_call" | custom-call | flops 1073741824 | bytes 1048576 | tf_op jit(solution)/shard_map/pallas_call | solution.py:246
  61.2 0.0 all-to-all-done
  61.3 2.4 %gather_fusion.1 = bf16[4,32,1024]{2,1,0:T(8,128)(2,1)} fusion(bf16[8,32,1024]{2,1,0:T(8,128)(2,1)} %all-to-all-done, s32[1024]{0:T(1024)} %pad_clamp_fusion), kind=kCustom, calls=%fused_computation.1 | custom fusion | bytes 524304 | tf_op jit(solution)/shard_map/gather | solution.py:224
  63.7 0.0 copy-start.2
  63.7 1.2 %fusion.2 = (f32[128,1024]{1,0:T(8,128)S(1)}, bf16[128,1024]{1,0:T(8,128)(2,1)S(1)}) fusion(f32[128,1024]{1,0:T(8,128)S(1)} %shard_map.95, bf16[128,1024]{1,0:T(8,128)(2,1)} %param.8, bf16[4,32,1024]{2,1,0:T(8,128)(2,1)} %gather_fusion.1, f32[3,128,1024]{2,1,0:T(8,128)S(1)} %get-tuple-element.11), kind=kLoop, calls=%fused_computation.7 | loop fusion | flops 786432 | bytes 2359296 | tf_op jit(solution)/shard_map/mul | solution.py:258
  64.9 1.3 %collective-permute-start.1 = (bf16[128,1024]{1,0:T(8,128)(2,1)S(1)}, bf16[128,1024]{1,0:T(8,128)(2,1)S(1)}, u32[]{:S(2)}, u32[]{:S(2)}) collective-permute-start(bf16[128,1024]{1,0:T(8,128)(2,1)S(1)} %get-tuple-element.20.dmix_ref), channel_id=1, source_target_pairs={{4,0},{8,4},{12,8},{16,12},{20,16},{24,20},{28,24},{5,1},{9,5},{13... | collective-permute-start | bytes 786440 | tf_op jit(solution)/shard_map/ppermute | solution.py:20
  66.2 0.0 copy-done.2
  66.2 0.1 pad.2.clone
  66.3 0.1 slice.29.streams_ref
  66.3 8.9 %collective-permute-done.1.after_ref = bf16[128,1024]{1,0:T(8,128)(2,1)S(1)} collective-permute-done((bf16[128,1024]{1,0:T(8,128)(2,1)S(1)}, bf16[128,1024]{1,0:T(8,128)(2,1)S(1)}, u32[]{:S(2)}, u32[]{:S(2)}) %collective-permute-start.1) | collective-permute-done | bytes 262176 | tf_op jit(solution)/shard_map/ppermute | solution.py:20
  75.2 7.4 %shard_map.96 = (f32[3,128,1024]{2,1,0:T(8,128)S(1)}, f32[64,128]{1,0:T(8,128)S(1)}, f32[3,7,1024]{2,1,0:T(8,128)S(1)}, bf16[3,8,1024]{2,1,0:T(8,128)(2,1)S(1)}) custom-call(f32[64,128]{1,0:T(8,128)S(1)} %convert_element_type.23.filt_ref, bf16[128,1024]{1,0:T(8,128)(2,1)S(1)} %get-tuple-element.20.dmix_ref, ...), custom_call_target="tpu_custom_call" | custom-call | flops 2147483648 | bytes 5242880 | tf_op jit(solution)/shard_map/pallas_call | solution.py:261
  82.7 0.4 fusion.1
  83.1 0.1 maximum_maximum_fusion
  83.2 17.2 %shard_map.97 = (bf16[3,128,1024]{2,1,0:T(8,128)(2,1)S(1)}, f32[8,11,128]{2,1,0:T(8,128)S(1)}) custom-call(f32[8,11,128]{2,1,0:T(8,128)S(1)} %reshape.109.part_ref, f32[3,128,1024]{2,1,0:T(8,128)S(1)} %get-tuple-element.15.ds_ref, bf16[3,8,1024]{2,1,0:T(8,128)(2,1)S(1)} %get-tuple-element.16.head_ref, f32[3,7,1024]{2,1,0:T(8,128)S(1)} %bitcast.28), custom_call_target="tpu_custom_call" | custom-call | flops 5505024 | bytes 2621440 | tf_op jit(solution)/shard_map/pallas_call | solution.py:294
  100.4 0.1 rev.4
  100.5 0.6 broadcast_multiply_fusion
  101.1 0.6 mul.28
  101.7 0.9 copy.12
  (15 shorter events, 0.1 us)
Async XLA Ops:
  7.2 30.9 %reduce-scatter.2.cloned.1.call-start = ((), (), s32[]{:S(2)}) async-start(), calls=%async_computation.2 | async-start | bytes 1310720 | tf_op jit(solution)/shard_map/reduce_scatter | solution.py:222
  7.2 39.1 %copy-start.3 = (bf16[3,64,7]{1,2,0:T(8,128)(2,1)S(1)}, bf16[3,64,7]{1,2,0:T(8,128)(2,1)}, u32[]{:S(2)}) copy-start(bf16[3,64,7]{1,2,0:T(8,128)(2,1)} %param.10) | copy-start | bytes 8068
  8.7 38.2 %collective-permute-start = (bf16[3,6,1024]{2,1,0:T(8,128)(2,1)S(1)}, bf16[3,6,1024]{2,1,0:T(8,128)(2,1)S(1)}, u32[]{:S(2)}, u32[]{:S(2)}) collective-permute-start(bf16[3,6,1024]{2,1,0:T(8,128)(2,1)S(1)} %slice.27), channel_id=1, source_target_pairs={{0,4},{4,8},{8,12},{12,16},{16,20},{20,24},{24,28},{1,5},{5,9},{9,... | collective-permute-start | bytes 110600 | tf_op jit(solution)/shard_map/ppermute | solution.py:20
  38.0 8.9 %copy-start = (bf16[3,128,1024]{2,1,0:T(8,128)(2,1)S(1)}, bf16[3,128,1024]{2,1,0:T(8,128)(2,1)}, u32[]{:S(2)}) copy-start(bf16[3,128,1024]{2,1,0:T(8,128)(2,1)} %feat_ref.3) | copy-start | bytes 2359300
  40.4 12.4 %copy-start.1 = (bf16[64,128]{1,0:T(8,128)(2,1)S(1)}, bf16[64,128]{1,0:T(8,128)(2,1)}, u32[]{:S(2)}) copy-start(bf16[64,128]{1,0:T(8,128)(2,1)} %param.11) | copy-start | bytes 49156
  40.4 20.8 %all-to-all-start = ((bf16[8,32,1024]{2,1,0:T(8,128)(2,1)}), bf16[8,32,1024]{2,1,0:T(8,128)(2,1)}, u32[]{:S(2)}, u32[]{:S(2)}) async-start(bf16[8,32,1024]{2,1,0:T(8,128)(2,1)} %gather_fusion), calls=%async_computation.1 | async-start | bytes 1048576 | tf_op jit(solution)/shard_map/all_to_all | solution.py:224
  48.9 10.2 %collective-permute-start.2 = (bf16[128,1024]{1,0:T(8,128)(2,1)S(1)}, bf16[128,1024]{1,0:T(8,128)(2,1)S(1)}, u32[]{:S(2)}, u32[]{:S(2)}) collective-permute-start(bf16[128,1024]{1,0:T(8,128)(2,1)S(1)} %get-tuple-element.12.own_ref.kv_ref), channel_id=1, source_target_pairs={{0,4},{4,8},{8,12},{12,16},{16,20},{20,24},{24,28},{1,5},{5,9},{9,... | collective-permute-start | bytes 786440 | tf_op jit(solution)/shard_map/ppermute | solution.py:20
  63.7 2.5 %copy-start.2 = (bf16[64,128]{1,0:T(8,128)(2,1)S(1)}, bf16[64,128]{1,0:T(8,128)(2,1)}, u32[]{:S(2)}) copy-start(bf16[64,128]{1,0:T(8,128)(2,1)} %param.11) | copy-start | bytes 49156
  64.9 10.4 %collective-permute-start.1 = (bf16[128,1024]{1,0:T(8,128)(2,1)S(1)}, bf16[128,1024]{1,0:T(8,128)(2,1)S(1)}, u32[]{:S(2)}, u32[]{:S(2)}) collective-permute-start(bf16[128,1024]{1,0:T(8,128)(2,1)S(1)} %get-tuple-element.20.dmix_ref), channel_id=1, source_target_pairs={{4,0},{8,4},{12,8},{16,12},{20,16},{24,20},{28,24},{5,1},{9,5},{13... | collective-permute-start | bytes 786440 | tf_op jit(solution)/shard_map/ppermute | solution.py:20
Sparse Core Ops, SparseCore 0:
  10.5 27.4 reduce-scatter.1

commit v3 on v2

--- a/solution.py
+++ b/solution.py
@@ -37,41 +37,174 @@
     )
 
 
-def streams_kernel(feat_ref, rim_ref, wt_ref, streams_ref, kv_ref, ext):
-    rows = feat_ref.shape[1]
-    taps = wt_ref.shape[1]
-    found = []
-    for s in range(3):
-        ext[8 - taps + 1 : 8] = rim_ref[s].astype(jnp.float32)
-        ext[8:] = feat_ref[s].astype(jnp.float32)
-        total = wt_ref[s, 0:1, :] * ext[8:]
-        for lag in range(1, taps):
-            total = total + wt_ref[s, lag : lag + 1, :] * ext[8 - lag : 8 - lag + rows]
-        streams_ref[s] = total
-        found.append(total)
-    kv_ref[...] = (found[1] * found[2]).astype(kv_ref.dtype)
-
-
 def plane(rows, axis):
     return lax.broadcasted_iota(jnp.int32, (rows, rows), axis)
 
 
-def mixed_kernel(filt_ref, before_ref, own_ref, mixed_ref):
-    taps = filt_ref.shape[1]
-    width = own_ref.shape[1]
-    window = jnp.concatenate([before_ref[...], own_ref[...]], axis=0)
-    t, s = plane(taps, 0), plane(taps, 1)
-    owner = lax.broadcasted_iota(jnp.int32, (taps, width), 1) // GROUP
-    total = jnp.zeros((taps, width), jnp.float32)
-    for g in range(width // GROUP):
-        line = jnp.broadcast_to(filt_ref[g : g + 1, :], (taps, taps))
-        wheel = pltpu.roll(line, 0, 1, stride=1, stride_axis=0)
-        table = jnp.concatenate(
-            [jnp.where(s > t, wheel, 0.0), jnp.where(s <= t, wheel, 0.0)], axis=1
-        ).astype(own_ref.dtype)
-        product = jnp.dot(table, window, preferred_element_type=jnp.float32)
-        total = jnp.where(owner == g, product, total)
-    mixed_ref[...] = total
+def front_kernel(
+    n, tp, pick_ref, origin_ref, attn_ref, feat_ref, out_grad_ref, wt_ref, filt_ref,
+    streams_ref, kv_ref, before_ref, rim_ref, dmix_ref, dq_ref, after_ref,
+    got, passed, crossed, acc, pieces, stage, landed, rim_in, key_in, mix_in, ext,
+    pair_send, pair_recv, cross_send, cross_recv, send, recv, halo_send, halo_recv,
+):
+    me = lax.axis_index("ctx")
+    col = lax.axis_index("tp")
+    f32 = jnp.float32
+    rows, width = kv_ref.shape
+    taps = wt_ref.shape[1]
+    long_taps = filt_ref.shape[1]
+    chunk = ext.shape[1]
+    piece_rows = stage.shape[1]
+    half = tp // 2
+    blocks = got.shape[1]
+    part = rows // blocks
+    side, row = lax.rem(col, 2), col // 2
+    partner = row * 2 + 1 - side
+    barrier = pltpu.get_barrier_semaphore()
+
+    def other(d):
+        return lax.rem(row + d, half) * 2 + side
+
+    def greet(k, carry):
+        pl.semaphore_signal(
+            barrier, inc=1, device_id={"ctx": lax.rem(me + k, n)}, device_id_type=MESH
+        )
+        return carry
+
+    lax.fori_loop(1, n, greet, 0)
+    pl.semaphore_signal(barrier, inc=1, device_id={"tp": partner}, device_id_type=MESH)
+    for d in range(1, half):
+        pl.semaphore_signal(barrier, inc=1, device_id={"tp": other(d)}, device_id_type=MESH)
+    pl.semaphore_wait(barrier, n - 1 + half)
+
+    def hop(source, target, at, by):
+        return pltpu.make_async_remote_copy(
+            source, target, halo_send.at[at], halo_recv.at[at],
+            device_id={"ctx": lax.rem(me + by + n, n)}, device_id_type=MESH,
+        )
+
+    def slab(which, r):
+        lane = pl.multiple_of(which * width, width)
+        return attn_ref.at[pl.ds(r * part, part), pl.ds(lane, width)]
+
+    def slab_value(which, r):
+        lane = pl.multiple_of(which * width, width)
+        return attn_ref[pl.ds(r * part, part), pl.ds(lane, width)].astype(f32)
+
+    def pair(d, r):
+        line = lax.rem(row + d, half)
+        return pltpu.make_async_remote_copy(
+            slab(line * 2 + 1 - side, r), got.at[d, r],
+            pair_send.at[d, r], pair_recv.at[d, r],
+            device_id={"tp": partner}, device_id_type=MESH,
+        )
+
+    def cross(d, r):
+        return pltpu.make_async_remote_copy(
+            passed.at[d, r], crossed.at[d, r], cross_send.at[d, r], cross_recv.at[d, r],
+            device_id={"tp": other(d)}, device_id_type=MESH,
+        )
+
+    order = [d for d in range(1, half)] + [0]
+    rim_hop = hop(feat_ref.at[:, pl.ds(rows - 16, 16), :], rim_in, 0, 1)
+    rim_hop.start()
+    for d in order:
+        for r in range(blocks):
+            pair(d, r).start()
+    for d in range(1, half):
+        for r in range(blocks):
+            pair(d, r).wait()
+            passed[d, r] = (slab_value(other(d), r) + got[d, r].astype(f32)).astype(got.dtype)
+            cross(d, r).start()
+    rim_hop.wait()
+    first = me == 0
+    last = me == n - 1
+    rim_ref[...] = jnp.where(first, 0.0, rim_in[...].astype(f32)).astype(rim_ref.dtype)
+
+    def stream_step(c, carry):
+        cols = pl.ds(pl.multiple_of(c * chunk, chunk), chunk)
+        found = []
+        for s in range(3):
+            ext[0:16] = rim_ref[s, :, cols].astype(f32)
+            ext[16:] = feat_ref[s, :, cols].astype(f32)
+            total = wt_ref[s, 0:1, cols] * ext[16:]
+            for lag in range(1, taps):
+                total = total + wt_ref[s, lag : lag + 1, cols] * ext[16 - lag : 16 - lag + rows]
+            streams_ref[s, :, cols] = total
+            found.append(total)
+        kv_ref[:, cols] = (found[1] * found[2]).astype(kv_ref.dtype)
+        return carry
+
+    lax.fori_loop(0, width // chunk, stream_step, 0)
+    key_hop = hop(kv_ref, key_in, 1, 1)
+    key_hop.start()
+    for r in range(blocks):
+        pair(0, r).wait()
+        total = slab_value(col, r) + got[0, r].astype(f32)
+        for d in range(1, half):
+            cross(d, r).wait()
+            total = total + crossed[d, r].astype(f32)
+        for i in range(part // piece_rows):
+            pieces[r * (part // piece_rows) + i] = total[i * piece_rows : (i + 1) * piece_rows]
+
+    def route(k):
+        peer = lax.rem(me + k, n)
+        return pltpu.make_async_remote_copy(
+            stage.at[k], landed.at[k], send.at[k], recv.at[k],
+            device_id={"ctx": peer}, device_id_type=MESH,
+        )
+
+    def piece(k):
+        slot = pick_ref[lax.rem(me + k, n)]
+        return pieces[slot].astype(stage.dtype)
+
+    def send_step(k, carry):
+        stage[k] = piece(k)
+        route(k).start()
+        return carry
+
+    lax.fori_loop(1, n, send_step, 0)
+    landed[0] = piece(0)
+    key_hop.wait()
+    before_ref[...] = jnp.where(first, 0.0, key_in[...].astype(f32)).astype(before_ref.dtype)
+    t, s = plane(long_taps, 0), plane(long_taps, 1)
+    owner = lax.broadcasted_iota(jnp.int32, (long_taps, chunk), 1) // GROUP
+
+    def mixed_step(c, carry):
+        cols = pl.ds(pl.multiple_of(c * chunk, chunk), chunk)
+        window = jnp.concatenate([before_ref[:, cols], kv_ref[:, cols]], axis=0)
+        total = jnp.zeros((long_taps, chunk), f32)
+        for g in range(chunk // GROUP):
+            line = jnp.broadcast_to(
+                filt_ref[pl.ds(c * (chunk // GROUP) + g, 1), :], (long_taps, long_taps)
+            )
+            wheel = pltpu.roll(line, 0, 1, stride=1, stride_axis=0)
+            table = jnp.concatenate(
+                [jnp.where(s > t, wheel, 0.0), jnp.where(s <= t, wheel, 0.0)], axis=1
+            ).astype(kv_ref.dtype)
+            product = jnp.dot(table, window, preferred_element_type=f32)
+            total = jnp.where(owner == g, product, total)
+        dq_ref[:, cols] = total
+        return carry
+
+    lax.fori_loop(0, width // chunk, mixed_step, 0)
+
+    def wait_step(k, carry):
+        route(k).wait()
+        return carry
+
+    lax.fori_loop(1, n, wait_step, 0)
+
+    for slot in range(rows // piece_rows):
+        at = lax.rem(me - origin_ref[slot] + n, n)
+        acc[slot * piece_rows : (slot + 1) * piece_rows] = landed[at].astype(f32)
+    grad = out_grad_ref[...].astype(f32) + acc[...]
+    dmix_ref[...] = (grad * streams_ref[0]).astype(dmix_ref.dtype)
+    mix_hop = hop(dmix_ref, mix_in, 2, -1)
+    mix_hop.start()
+    dq_ref[...] = grad * dq_ref[...]
+    mix_hop.wait()
+    after_ref[...] = jnp.where(last, 0.0, mix_in[...].astype(f32)).astype(after_ref.dtype)
 
 
 def back_kernel(
@@ -110,11 +243,11 @@
     for k in range(3):
         dstreams_ref[k] = parts[k]
         head_ref[k] = parts[k][:8].astype(head_ref.dtype)
-        ext[8 - short_taps + 1 : 8] = rim_ref[k].astype(jnp.float32)
-        ext[8:] = feat_ref[k].astype(jnp.float32)
+        ext[0:16] = rim_ref[k].astype(jnp.float32)
+        ext[16:] = feat_ref[k].astype(jnp.float32)
         for lag in range(short_taps):
             short_ref[k, lag : lag + 1, :] = jnp.sum(
-                parts[k] * ext[8 - lag : 8 - lag + rows], axis=0, keepdims=True
+                parts[k] * ext[16 - lag : 16 - lag + rows], axis=0, keepdims=True
             )
 
 
@@ -219,44 +352,51 @@
     keyed = jnp.where(everyone == own_index, positions, -1)
     hits = jnp.any(keyed[:, :, None] == slot_ids[None, None, :], axis=1)
     source_of = jnp.sum(jnp.where(hits, device_ids[:, None], 0), axis=0)
-    summed = lax.psum_scatter(attn_parts[0], "tp", scatter_dimension=1, tiled=True)
-    pieces = summed.reshape(per_device, piece_rows, -1)
-    attn_home = lax.all_to_all(
-        pieces[send_slot], "ctx", split_axis=0, concat_axis=0, tiled=True
-    )[source_of].reshape(rows, -1)
-
     short_weights = jnp.transpose(jnp.repeat(short_filt, GROUP, axis=1), (0, 2, 1)).astype(f32)
     filt = med_filt.astype(f32)
     filt_back = jnp.roll(filt[:, ::-1], 1, axis=1)
-    stream_rim = shifted(features[:, rows - short_taps + 1 :, :], "ctx", 1)
-    streams, keyval = call(
-        streams_kernel,
-        grid,
-        [lead3(rows), lead3(short_taps - 1), lead3(short_taps)],
-        (lead3(rows), flat(rows)),
-        (
+    tp_count = lax.axis_size("tp")
+    blocks = 2 if rows % 32 == 0 else 1
+    vmem = pl.BlockSpec(memory_space=pltpu.VMEM)
+    smem = pl.BlockSpec(memory_space=pltpu.SMEM)
+    dma = pltpu.SemaphoreType.DMA
+    lanes = jax.ShapeDtypeStruct((rows, width), half)
+    crossing = pltpu.VMEM((tp_count // 2, blocks, rows // blocks, width), half)
+    flags = dma((tp_count // 2, blocks))
+    routed = pltpu.VMEM((ctx_count, piece_rows, width), half)
+    streams, keyval, key_rim, stream_rim, dmix, dquery, grad_rim = pl.pallas_call(
+        functools.partial(front_kernel, ctx_count, tp_count),
+        in_specs=[smem, smem] + [vmem] * 5,
+        out_specs=(vmem,) * 7,
+        out_shape=(
             jax.ShapeDtypeStruct((3, rows, width), f32),
-            jax.ShapeDtypeStruct((rows, width), half),
-        ),
-        3 * 14 * rows * width,
-        20 * rows * width,
-        [pltpu.VMEM((rows + 8, chunk), f32)],
-    )(features, stream_rim, short_weights)
-    key_rim = shifted(keyval, "ctx", 1)
-    mixed = call(
-        mixed_kernel,
-        grid,
-        [filt_spec, flat(rows), flat(rows)],
-        flat(rows),
-        jax.ShapeDtypeStruct((rows, width), f32),
-        4 * groups * taps * taps * chunk,
-        8 * rows * width,
-    )(filt_back, key_rim, keyval)
-
-    grad = out_grad.astype(f32) + attn_home.astype(f32)
-    dmix = (grad * streams[0]).astype(half)
-    dquery = grad * mixed
-    grad_rim = shifted(dmix, "ctx", -1)
+            lanes,
+            lanes,
+            jax.ShapeDtypeStruct((3, 16, width), half),
+            lanes,
+            jax.ShapeDtypeStruct((rows, width), f32),
+            lanes,
+        ),
+        scratch_shapes=[
+            crossing, crossing, crossing,
+            pltpu.VMEM((rows, width), f32),
+            pltpu.VMEM((per_device, piece_rows, width), f32),
+            routed, routed,
+            pltpu.VMEM((3, 16, width), half),
+            pltpu.VMEM((rows, width), half),
+            pltpu.VMEM((rows, width), half),
+            pltpu.VMEM((rows + 16, chunk), f32),
+            flags, flags, flags, flags,
+            dma((ctx_count,)), dma((ctx_count,)), dma((3,)), dma((3,)),
+        ],
+        compiler_params=pltpu.CompilerParams(
+            collective_id=0, has_side_effects=True, vmem_limit_bytes=48 * 1024 * 1024
+        ),
+        cost_estimate=cost(4 * groups * taps * taps * chunk, 40 * rows * width),
+    )(
+        send_slot.astype(jnp.int32), source_of.astype(jnp.int32), attn_parts[0], features,
+        out_grad, short_weights, filt_back,
+    )
     pair = streams[1:]
     dstreams, med_part, short_cols, heads = call(
         back_kernel,
@@ -264,7 +404,7 @@
         [
             filt_spec, flat(rows), flat(rows), flat(rows), flat(rows),
             pl.BlockSpec((2, rows, chunk), lambda i: (0, 0, i)),
-            flat(rows), lead3(rows), lead3(short_taps - 1),
+            flat(rows), lead3(rows), lead3(16),
         ],
         (lead3(rows), filt_spec, lead3(short_taps), lead3(8)),
         (
@@ -275,7 +415,7 @@
         ),
         8 * groups * taps * taps * chunk,
         40 * rows * width,
-        [pltpu.VMEM((rows + 8, chunk), f32)],
+        [pltpu.VMEM((rows + 16, chunk), f32)],
     )(filt, dmix, grad_rim, keyval, key_rim, pair, dquery, features, stream_rim)
     member = (
         jnp.arange(width, dtype=jnp.int32)[:, None] // GROUP

time: 110 us -> 69.4 us (0.63)
  waiting for transfers between devices: 37.8 us -> 0 us
  Pallas kernels: 28.7 us -> 59.2 us
  starting transfers between devices: 15.8 us -> 0 us
  between operations: 14.2 us -> 0.8 us
  local copies, waits for them, and re-layouts: 9.04 us -> 7.1 us
  other arithmetic: 3.48 us -> 1.62 us
    pallas_call x2 -> x1, Pallas kernels: 4.1 us -> 34.2 us  [shards(): pl.pallas_call(functools.partial(front_kernel, ctx_count, tp_count), in_s...]
    reduce_scatter x1 -> x0, waiting for transfers between devices: 22.8 us -> none  [shards(): lax.psum_scatter(attn_parts[0], 'tp', scatter_dimension=1, tiled=True)]
    ppermute x3 -> x0, waiting for transfers between devices: 14.3 us -> none  [shifted(): return lax.ppermute(x, axis, pairs)]
    ppermute x3 -> x0, starting transfers between devices: 10.1 us -> none  [shifted(): return lax.ppermute(x, axis, pairs)]
    all_to_all x1 -> x0, starting transfers between devices: 5.65 us -> none  [shards(): lax.all_to_all(pieces[send_slot], 'ctx', split_axis=0, concat_axis=0, til...]
    gather x2 -> x0, local copies, waits for them, and re-layouts: 4.82 us -> none  [the longest x1 2.43 us: shards(): lax.all_to_all(pieces[send_slot], 'ctx', split_axis=0, concat_axis=0, til...]
    unnamed x9 -> x11, local copies, waits for them, and re-layouts: 0.89 us -> 3.06 us
    mul x1 -> x0, other arithmetic: 1.17 us -> none  [shards(): dquery = grad * mixed]
  transfers between devices with their start and end apart: 5 -> 0, of which waited for: 3 -> 0; matrix products, arithmetic and copies ran while one was open for 6% -> 0% of each run, Pallas kernels for 4% -> 0%
where the time goes in v3:
time: 69.4 us; the launch traced here: 69.1 us
  Pallas kernels  59.2 us (85%)
  local copies, waits for them, and re-layouts  7.1 us (10%)
  other arithmetic  1.62 us (2%)
  between operations  0.8 us (1%)
    pallas_call x1, Pallas kernels, shards(): pl.pallas_call(functools.partial(front_kernel, ctx_count, tp_count), in_s...  34.2 us
    pallas_call x1, Pallas kernels, shards(): pl.pallas_call(functools.partial(final_kernel, ctx_count), in_specs=[vmem...  17.7 us
    pallas_call x1, Pallas kernels, shards(): call(back_kernel, grid, [filt_spec, flat(rows), flat(rows), flat(rows), f...  7.38 us
    unnamed x11, local copies, waits for them, and re-layouts  3.06 us

profile of v3, /device:TPU:0, one launch (start us, length us, event | category | flops | bytes accessed | tf_op | source)
XLA Modules:
  0.0 69.1 jit_solution(9416005436833408649)
XLA Ops:
  0.6 0.0 copy-start.4
  0.6 0.0 copy-start
  0.7 0.0 copy-start.3
  0.7 0.8 %reshape.73 = s32[8,4]{1,0:T(8,128)S(1)} reshape(s32[32]{0:T(128)} %param.12) | data formatting | bytes 256 | tf_op jit(solution)/shard_map/reshape | solution.py:345
  1.5 0.7 and_select_fusion
  2.2 0.1 reshape.74
  2.3 0.1 copy.10
  2.4 0.1 select_reduce_fusion
  2.5 0.9 %broadcast_in_dim.40 = f32[3,64,16,7]{2,1,3,0:T(8,128)S(1)} broadcast(bf16[3,64,7]{1,2,0:T(8,128)(2,1)} %param.10), dimensions={0,1,3} | broadcast | bytes 88704 | tf_op jit(solution)/shard_map/broadcast_in_dim | solution.py:355
  3.4 0.4 convert_element_type.13
  3.8 0.8 %slice.28 = f32[64,127]{1,0:T(8,128)S(1)} slice(bf16[64,128]{1,0:T(8,128)(2,1)} %param.11), slice={[0:64], [1:128]} | slice | bytes 65024 | tf_op jit(solution)/shard_map/jit(_roll_static)/slice | solution.py:357
  4.6 0.1 slice.23
  4.7 0.0 copy-done.4
  4.7 0.1 pad_maximum_fusion.filt_ref
  4.8 0.0 copy-done
  4.8 0.0 copy-done.3
  4.8 0.0 copy-start.1
  4.8 1.1 %copy-done.1 = bf16[3,128,1024]{2,1,0:T(8,128)(2,1)S(1)} copy-done((bf16[3,128,1024]{2,1,0:T(8,128)(2,1)S(1)}, bf16[3,128,1024]{2,1,0:T(8,128)(2,1)}, u32[]{:S(2)}) %copy-start.1) | copy-done | bytes 786456
  5.9 34.2 %shard_map.94 = (f32[3,128,1024]{2,1,0:T(8,128)S(1)}, bf16[128,1024]{1,0:T(8,128)(2,1)S(1)}, bf16[128,1024]{1,0:T(8,128)(2,1)S(1)}, bf16[3,16,1024]{2,1,0:T(8,12...) custom-call(s32[8]{0:T(128)S(1)} %get-tuple-element.30.pick_ref, ...), custom_call_target="tpu_custom_call" | custom-call | flops 1073741824 | bytes 5242880 | tf_op jit(solution)/shard_map/pallas_call | solution.py:367
  40.1 0.0 copy-start.2
  40.1 0.1 slice.24.streams_ref
  40.2 1.0 %copy-done.2 = bf16[3,128,1024]{2,1,0:T(8,128)(2,1)S(1)} copy-done((bf16[3,128,1024]{2,1,0:T(8,128)(2,1)S(1)}, bf16[3,128,1024]{2,1,0:T(8,128)(2,1)}, u32[]{:S(2)}) %copy-start.2) | copy-done | bytes 786456
  41.2 7.4 %shard_map.95 = (f32[3,128,1024]{2,1,0:T(8,128)S(1)}, f32[64,128]{1,0:T(8,128)S(1)}, f32[3,7,1024]{2,1,0:T(8,128)S(1)}, bf16[3,8,1024]{2,1,0:T(8,128)(2,1)S(1)}) custom-call(f32[64,128]{1,0:T(8,128)S(1)} %convert_element_type.11.filt_ref, bf16[128,1024]{1,0:T(8,128)(2,1)S(1)} %get-tuple-element.16.dmix_ref, ...), custom_call_target="tpu_custom_call" | custom-call | flops 2147483648 | bytes 5242880 | tf_op jit(solution)/shard_map/pallas_call | solution.py:401
  48.6 0.4 fusion
  49.0 0.1 pad.2.clone
  49.1 0.1 maximum_maximum_fusion
  49.2 17.7 %shard_map.96 = (bf16[3,128,1024]{2,1,0:T(8,128)(2,1)S(1)}, f32[8,11,128]{2,1,0:T(8,128)S(1)}) custom-call(f32[8,11,128]{2,1,0:T(8,128)S(1)} %reshape.76.part_ref, f32[3,128,1024]{2,1,0:T(8,128)S(1)} %get-tuple-element.25.ds_ref, bf16[3,8,1024]{2,1,0:T(8,128)(2,1)S(1)} %get-tuple-element.26.head_ref, f32[3,7,1024]{2,1,0:T(8,128)S(1)} %bitcast.11), custom_call_target="tpu_custom_call" | custom-call | flops 5505024 | bytes 2621440 | tf_op jit(solution)/shard_map/pallas_call | solution.py:434
  66.9 0.1 rev.4
  67.0 0.6 broadcast_multiply_fusion
  67.6 0.6 mul.20
  68.2 0.9 %copy.12 = bf16[3,128,1024]{2,1,0:T(8,128)(2,1)} copy(bf16[3,128,1024]{2,1,0:T(8,128)(2,1)S(1)} %get-tuple-element.34) | data formatting | bytes 1572864
  (12 shorter events, 0.1 us)
Async XLA Ops:
  0.6 4.1 %copy-start.4 = (bf16[64,128]{1,0:T(8,128)(2,1)S(1)}, bf16[64,128]{1,0:T(8,128)(2,1)}, u32[]{:S(2)}) copy-start(bf16[64,128]{1,0:T(8,128)(2,1)} %param.11) | copy-start | bytes 49156
  0.6 4.1 %copy-start = (bf16[1,128,4096]{2,1,0:T(8,128)(2,1)S(1)}, bf16[1,128,4096]{2,1,0:T(8,128)(2,1)}, u32[]{:S(2)}) copy-start(bf16[1,128,4096]{2,1,0:T(8,128)(2,1)} %param.9) | copy-start | bytes 3145732
  0.7 4.1 %copy-start.3 = (bf16[128,1024]{1,0:T(8,128)(2,1)S(1)}, bf16[128,1024]{1,0:T(8,128)(2,1)}, u32[]{:S(2)}) copy-start(bf16[128,1024]{1,0:T(8,128)(2,1)} %out_grad_ref.1) | copy-start | bytes 786436
  4.8 1.1 %copy-start.1 = (bf16[3,128,1024]{2,1,0:T(8,128)(2,1)S(1)}, bf16[3,128,1024]{2,1,0:T(8,128)(2,1)}, u32[]{:S(2)}) copy-start(bf16[3,128,1024]{2,1,0:T(8,128)(2,1)} %feat_ref.3) | copy-start | bytes 2359300
  40.1 1.1 %copy-start.2 = (bf16[3,128,1024]{2,1,0:T(8,128)(2,1)S(1)}, bf16[3,128,1024]{2,1,0:T(8,128)(2,1)}, u32[]{:S(2)}) copy-start(bf16[3,128,1024]{2,1,0:T(8,128)(2,1)} %feat_ref.3) | copy-start | bytes 2359300

commit v4 on v3

v4 whole, which is shorter than its diff:
```python
import functools
import math

import jax
import jax.numpy as jnp
from jax import lax
from jax.experimental import pallas as pl
from jax.experimental.pallas import tpu as pltpu
from jax.sharding import PartitionSpec as P

GROUP = 16
MESH = pl.DeviceIdType.MESH
LANES = 256


def cost(flops, bytes_accessed):
    return pl.CostEstimate(flops=flops, bytes_accessed=bytes_accessed, transcendentals=0)


def plane(rows, axis):
    return lax.broadcasted_iota(jnp.int32, (rows, rows), axis)


def whole_kernel(
    n, tp, pick_ref, origin_ref, attn_ref, feat_ref, out_grad_ref, wt_ref, filt_ref, back_ref,
    feat_out, total_ref,
    streams_ref, kv_ref, before_ref, rim_ref, dmix_ref, ds_ref, after_ref,
    short_ref, flat_ref, part_ref, sums, gathered, head_ref, tail_in,
    got, passed, crossed, acc, pieces, stage, landed, rim_in, key_in, mix_in, ext,
    pair_send, pair_recv, cross_send, cross_recv, send, recv, halo_send, halo_recv,
    send1, recv1, send2, recv2,
):
    dq_ref = ds_ref.at[0]
    me = lax.axis_index("ctx")
    col = lax.axis_index("tp")
    f32 = jnp.float32
    rows, width = kv_ref.shape
    taps = wt_ref.shape[1]
    long_taps = filt_ref.shape[1]
    chunk = ext.shape[1]
    piece_rows = stage.shape[1]
    half = tp // 2
    blocks = got.shape[1]
    part = rows // blocks
    side, row = lax.rem(col, 2), col // 2
    partner = row * 2 + 1 - side
    barrier = pltpu.get_barrier_semaphore()

    def other(d):
        return lax.rem(row + d, half) * 2 + side

    def greet(k, carry):
        pl.semaphore_signal(
            barrier, inc=1, device_id={"ctx": lax.rem(me + k, n)}, device_id_type=MESH
        )
        return carry

    lax.fori_loop(1, n, greet, 0)
    pl.semaphore_signal(barrier, inc=1, device_id={"tp": partner}, device_id_type=MESH)
    for d in range(1, half):
        pl.semaphore_signal(barrier, inc=1, device_id={"tp": other(d)}, device_id_type=MESH)
    pl.semaphore_wait(barrier, n - 1 + half)

    def hop(source, target, at, by):
        return pltpu.make_async_remote_copy(
            source, target, halo_send.at[at], halo_recv.at[at],
            device_id={"ctx": lax.rem(me + by + n, n)}, device_id_type=MESH,
        )

    def slab(which, r):
        lane = pl.multiple_of(which * width, width)
        return attn_ref.at[pl.ds(r * part, part), pl.ds(lane, width)]

    def slab_value(which, r):
        lane = pl.multiple_of(which * width, width)
        return attn_ref[pl.ds(r * part, part), pl.ds(lane, width)].astype(f32)

    def pair(d, r):
        line = lax.rem(row + d, half)
        return pltpu.make_async_remote_copy(
            slab(line * 2 + 1 - side, r), got.at[d, r],
            pair_send.at[d, r], pair_recv.at[d, r],
            device_id={"tp": partner}, device_id_type=MESH,
        )

    def cross(d, r):
        return pltpu.make_async_remote_copy(
            passed.at[d, r], crossed.at[d, r], cross_send.at[d, r], cross_recv.at[d, r],
            device_id={"tp": other(d)}, device_id_type=MESH,
        )

    order = [d for d in range(1, half)] + [0]
    rim_hop = hop(feat_ref.at[:, pl.ds(rows - 16, 16), :], rim_in, 0, 1)
    rim_hop.start()
    for d in order:
        for r in range(blocks):
            pair(d, r).start()
    for d in range(1, half):
        for r in range(blocks):
            pair(d, r).wait()
            passed[d, r] = (slab_value(other(d), r) + got[d, r].astype(f32)).astype(got.dtype)
            cross(d, r).start()
    rim_hop.wait()
    first = me == 0
    last = me == n - 1
    rim_ref[...] = jnp.where(first, 0.0, rim_in[...].astype(f32)).astype(rim_ref.dtype)

    def stream_step(c, carry):
        cols = pl.ds(pl.multiple_of(c * chunk, chunk), chunk)
        found = []
        for s in range(3):
            ext[0:16] = rim_ref[s, :, cols].astype(f32)
            ext[16:] = feat_ref[s, :, cols].astype(f32)
            total = wt_ref[s, 0:1, cols] * ext[16:]
            for lag in range(1, taps):
                total = total + wt_ref[s, lag : lag + 1, cols] * ext[16 - lag : 16 - lag + rows]
            streams_ref[s, :, cols] = total
            found.append(total)
        kv_ref[:, cols] = (found[1] * found[2]).astype(kv_ref.dtype)
        return carry

    lax.fori_loop(0, width // chunk, stream_step, 0)
    key_hop = hop(kv_ref, key_in, 1, 1)
    key_hop.start()
    for r in range(blocks):
        pair(0, r).wait()
        total = slab_value(col, r) + got[0, r].astype(f32)
        for d in range(1, half):
            cross(d, r).wait()
            total = total + crossed[d, r].astype(f32)
        for i in range(part // piece_rows):
            pieces[r * (part // piece_rows) + i] = total[i * piece_rows : (i + 1) * piece_rows]

    def route(k):
        peer = lax.rem(me + k, n)
        return pltpu.make_async_remote_copy(
            stage.at[k], landed.at[k], send.at[k], recv.at[k],
            device_id={"ctx": peer}, device_id_type=MESH,
        )

    def piece(k):
        slot = pick_ref[lax.rem(me + k, n)]
        return pieces[slot].astype(stage.dtype)

    def send_step(k, carry):
        stage[k] = piece(k)
        route(k).start()
        return carry

    lax.fori_loop(1, n, send_step, 0)
    landed[0] = piece(0)
    key_hop.wait()
    before_ref[...] = jnp.where(first, 0.0, key_in[...].astype(f32)).astype(before_ref.dtype)
    t, s = plane(long_taps, 0), plane(long_taps, 1)
    owner = lax.broadcasted_iota(jnp.int32, (long_taps, chunk), 1) // GROUP

    def mixed_step(c, carry):
        cols = pl.ds(pl.multiple_of(c * chunk, chunk), chunk)
        window = jnp.concatenate([before_ref[:, cols], kv_ref[:, cols]], axis=0)
        total = jnp.zeros((long_taps, chunk), f32)
        for g in range(chunk // GROUP):
            line = jnp.broadcast_to(
                filt_ref[pl.ds(c * (chunk // GROUP) + g, 1), :], (long_taps, long_taps)
            )
            wheel = pltpu.roll(line, 0, 1, stride=1, stride_axis=0)
            table = jnp.concatenate(
                [jnp.where(s > t, wheel, 0.0), jnp.where(s <= t, wheel, 0.0)], axis=1
            ).astype(kv_ref.dtype)
            product = jnp.dot(table, window, preferred_element_type=f32)
            total = jnp.where(owner == g, product, total)
        dq_ref[:, cols] = total
        return carry

    lax.fori_loop(0, width // chunk, mixed_step, 0)

    def wait_step(k, carry):
        route(k).wait()
        return carry

    lax.fori_loop(1, n, wait_step, 0)

    for slot in range(rows // piece_rows):
        at = lax.rem(me - origin_ref[slot] + n, n)
        acc[slot * piece_rows : (slot + 1) * piece_rows] = landed[at].astype(f32)
    grad = out_grad_ref[...].astype(f32) + acc[...]
    dmix_ref[...] = (grad * streams_ref[0]).astype(dmix_ref.dtype)
    mix_hop = hop(dmix_ref, mix_in, 2, -1)
    mix_hop.start()
    dq_ref[...] = grad * dq_ref[...]
    kind = dmix_ref.dtype
    flip = jnp.where(t + s == long_taps - 1, 1.0, 0.0).astype(kind)
    near = chunk // GROUP

    def short_sums(k, cols, value):
        ext[0:16] = rim_ref[k, :, cols].astype(f32)
        ext[16:] = feat_ref[k, :, cols].astype(f32)
        for lag in range(taps):
            at = k * taps + lag
            short_ref[at : at + 1, cols] = jnp.sum(
                value * ext[16 - lag : 16 - lag + rows], axis=0, keepdims=True
            )

    def lag_step(c, carry):
        cols = pl.ds(pl.multiple_of(c * chunk, chunk), chunk)
        flipped = jnp.dot(flip, dmix_ref[:, cols], preferred_element_type=f32)
        window = jnp.concatenate([before_ref[:, cols], kv_ref[:, cols]], axis=0)
        for g in range(near):
            left = jnp.where(owner == g, flipped, 0.0).astype(kind)
            both = lax.dot_general(
                left, window, (((1,), (1,)), ((), ())), preferred_element_type=f32
            )
            ring = jnp.where(s + t <= long_taps - 1, both[:, long_taps:], both[:, :long_taps])
            ring = pltpu.roll(ring, 0, 1, stride=1, stride_axis=0)
            flat_ref[pl.ds(c * near + g, 1), :] = jnp.sum(ring, axis=0, keepdims=True)
        short_sums(0, cols, dq_ref[:, cols])
        return carry

    lax.fori_loop(0, width // chunk, lag_step, 0)
    mix_hop.wait()
    after_ref[...] = jnp.where(last, 0.0, mix_in[...].astype(f32)).astype(kind)

    def back_step(c, carry):
        cols = pl.ds(pl.multiple_of(c * chunk, chunk), chunk)
        window = jnp.concatenate([dmix_ref[:, cols], after_ref[:, cols]], axis=0)
        total = jnp.zeros((long_taps, chunk), f32)
        for g in range(near):
            line = jnp.broadcast_to(
                back_ref[pl.ds(c * near + g, 1), :], (long_taps, long_taps)
            )
            wheel = pltpu.roll(line, 0, 1, stride=1, stride_axis=0)
            table = jnp.concatenate(
                [jnp.where(s >= t, wheel, 0.0), jnp.where(s < t, wheel, 0.0)], axis=1
            ).astype(kind)
            product = jnp.dot(table, window, preferred_element_type=f32)
            total = jnp.where(owner == g, product, total)
        for k in (1, 2):
            value = total * streams_ref[3 - k, :, cols]
            ds_ref[k, :, cols] = value
            short_sums(k, cols, value)
        return carry

    lax.fori_loop(0, width // chunk, back_step, 0)
    head_ref[...] = ds_ref[:, 0:16, :].astype(kind)
    tail_hop = hop(head_ref, tail_in, 3, -1)
    tail_hop.start()
    groups = width // GROUP
    used = groups + 3 * taps
    member = jnp.where(
        lax.broadcasted_iota(jnp.int32, (width, long_taps), 0) // GROUP
        == lax.broadcasted_iota(jnp.int32, (width, long_taps), 1),
        1.0,
        0.0,
    )
    flat_ref[groups:used] = jnp.dot(
        short_ref[...], member, precision=lax.Precision.HIGHEST, preferred_element_type=f32
    )
    share = part_ref.shape[1]
    if n * share > used:
        flat_ref[used : n * share] = jnp.zeros((n * share - used, long_taps), f32)
    for k in range(n):
        part_ref[k] = flat_ref[k * share : (k + 1) * share]

    def scatter(k):
        peer = lax.rem(me + k, n)
        return pltpu.make_async_remote_copy(
            part_ref.at[peer], sums.at[k], send1.at[k], recv1.at[k],
            device_id={"ctx": peer}, device_id_type=MESH,
        )

    def gather(k):
        return pltpu.make_async_remote_copy(
            gathered.at[me], gathered.at[me], send2.at[k], recv2.at[k],
            device_id={"ctx": lax.rem(me + k, n)}, device_id_type=MESH,
        )

    def each(copy, act):
        def step(k, carry):
            act(copy(k))
            return carry

        lax.fori_loop(1, n, step, 0)

    def feat_step(k):
        def step(c, carry):
            cols = pl.ds(pl.multiple_of(c * chunk, chunk), chunk)
            ext[0:rows] = ds_ref[k, :, cols]
            ext[rows:] = jnp.where(last, 0.0, tail_in[k, :, cols].astype(f32))
            total = wt_ref[k, 0:1, cols] * ds_ref[k, :, cols]
            for lag in range(1, taps):
                total = total + wt_ref[k, lag : lag + 1, cols] * ext[lag : lag + rows]
            feat_out[k, :, cols] = total.astype(feat_out.dtype)
            return carry

        lax.fori_loop(0, width // chunk, step, 0)

    each(scatter, lambda c: c.start())
    sums[0] = part_ref[me]
    tail_hop.wait()
    feat_step(0)
    each(scatter, lambda c: c.wait())
    result = sums[0]
    for k in range(1, n):
        result = result + sums[k]
    gathered[me] = result
    each(gather, lambda c: c.start())
    feat_step(1)
    feat_step(2)
    each(gather, lambda c: c.wait())
    total_ref[...] = gathered[...]


def shards(features, out_grad, attn_parts, short_filt, med_filt, piece_home, piece_start):
    rows, width = out_grad.shape
    groups, taps = med_filt.shape
    short_taps = short_filt.shape[2]
    ctx_count = lax.axis_size("ctx")
    own_index = lax.axis_index("ctx")
    per_device = ctx_count // 2
    piece_rows = rows // per_device
    factor = 1.0 / math.sqrt(rows * ctx_count * GROUP)
    chunk = LANES if width % LANES == 0 else width
    f32, half = jnp.float32, features.dtype

    everyone = piece_home.reshape(ctx_count, per_device)
    positions = (piece_start // piece_rows).reshape(ctx_count, per_device)
    local_home = lax.dynamic_slice_in_dim(everyone, own_index, 1, 0)[0]
    device_ids = jnp.arange(ctx_count, dtype=jnp.int32)
    slot_ids = jnp.arange(per_device, dtype=jnp.int32)
    matches = local_home[None, :] == device_ids[:, None]
    send_slot = jnp.sum(jnp.where(matches, slot_ids[None, :], 0), axis=1)
    keyed = jnp.where(everyone == own_index, positions, -1)
    hits = jnp.any(keyed[:, :, None] == slot_ids[None, None, :], axis=1)
    source_of = jnp.sum(jnp.where(hits, device_ids[:, None], 0), axis=0)
    short_weights = jnp.transpose(jnp.repeat(short_filt, GROUP, axis=1), (0, 2, 1)).astype(f32)
    filt = med_filt.astype(f32)
    filt_back = jnp.roll(filt[:, ::-1], 1, axis=1)
    tp_count = lax.axis_size("tp")
    blocks = 2 if rows % 32 == 0 else 1
    vmem = pl.BlockSpec(memory_space=pltpu.VMEM)
    smem = pl.BlockSpec(memory_space=pltpu.SMEM)
    dma = pltpu.SemaphoreType.DMA
    lanes = jax.ShapeDtypeStruct((rows, width), half)
    crossing = pltpu.VMEM((tp_count // 2, blocks, rows // blocks, width), half)
    flags = dma((tp_count // 2, blocks))
    routed = pltpu.VMEM((ctx_count, piece_rows, width), half)
    used = groups + 3 * short_taps
    share = -(-used // ctx_count)
    parts = (ctx_count, share, taps)
    held = pltpu.VMEM((rows, width), half)
    heads = pltpu.VMEM((3, 16, width), half)
    wide = pltpu.VMEM((3, rows, width), f32)
    peers = dma((ctx_count,))
    feat_grad, totals = pl.pallas_call(
        functools.partial(whole_kernel, ctx_count, tp_count),
        in_specs=[smem, smem] + [vmem] * 6,
        out_specs=(vmem, vmem),
        out_shape=(
            jax.ShapeDtypeStruct((3, rows, width), half),
            jax.ShapeDtypeStruct(parts, f32),
        ),
        scratch_shapes=[
            wide, held, held, heads, held, wide, held,
            pltpu.VMEM((3 * short_taps, width), f32),
            pltpu.VMEM((ctx_count * share, taps), f32),
            pltpu.VMEM(parts, f32), pltpu.VMEM(parts, f32), pltpu.VMEM(parts, f32),
            heads, heads,
            crossing, crossing, crossing,
            pltpu.VMEM((rows, width), f32),
            pltpu.VMEM((per_device, piece_rows, width), f32),
            routed, routed,
            heads, held, held,
            pltpu.VMEM((rows + 16, chunk), f32),
            flags, flags, flags, flags,
            peers, peers, dma((4,)), dma((4,)),
            peers, peers, peers, peers,
        ],
        compiler_params=pltpu.CompilerParams(
            collective_id=0, has_side_effects=True, vmem_limit_bytes=48 * 1024 * 1024
        ),
        cost_estimate=cost(12 * groups * taps * taps * chunk, 40 * rows * width),
    )(
        send_slot.astype(jnp.int32), source_of.astype(jnp.int32), attn_parts[0], features,
        out_grad, short_weights, filt_back, filt,
    )
    flat_totals = totals.reshape(-1, taps)
    short_total = flat_totals[groups:used, :groups].reshape(3, short_taps, groups)
    return (
        feat_grad,
        jnp.transpose(short_total, (0, 2, 1)) * factor,
        flat_totals[:groups, ::-1] * factor,
    )


def solution(mesh):
    return jax.shard_map(
        shards,
        mesh=mesh,
        in_specs=(
            P(None, "ctx", "tp"),
            P("ctx", "tp"),
            P("tp", "ctx", None),
            P(None, "tp", None),
            P("tp", None),
            P(),
            P(),
        ),
        out_specs=(P(None, "ctx", "tp"), P(None, "tp", None), P("tp", None)),
        check_vma=False,
    )
```

time: 69.4 us -> 61.5 us (0.89)
  Pallas kernels: 59.2 us -> 53.9 us
  local copies, waits for them, and re-layouts: 7.1 us -> 5.04 us
    pallas_call x3 -> x1, Pallas kernels: 59.2 us -> 53.9 us  [shards(): pl.pallas_call(functools.partial(whole_kernel, ctx_count, tp_count), in_s...]
    unnamed x11 -> x9, local copies, waits for them, and re-layouts: 3.06 us -> 1.84 us
    slice x3, local copies, waits for them, and re-layouts: 0.87 us -> 0.16 us  [shards(): filt_back = jnp.roll(filt[:, ::-1], 1, axis=1)]
where the time goes in v4:
time: 61.5 us; the launch traced here: 61.3 us
  Pallas kernels  53.9 us (88%)
  local copies, waits for them, and re-layouts  5.04 us (8%)
  other arithmetic  1.54 us (3%)
  between operations  0.73 us (1%)
    pallas_call x1, Pallas kernels, shards(): pl.pallas_call(functools.partial(whole_kernel, ctx_count, tp_count), in_s...  53.9 us
    unnamed x9, local copies, waits for them, and re-layouts  1.84 us

profile of v4, /device:TPU:0, one launch (start us, length us, event | category | flops | bytes accessed | tf_op | source)
XLA Modules:
  0.0 61.3 jit_solution(1024370978288653382)
XLA Ops:
  0.6 0.0 copy-start
  0.6 0.8 %reshape.30 = s32[8,4]{1,0:T(8,128)S(1)} reshape(s32[32]{0:T(128)} %param.12) | data formatting | bytes 256 | tf_op jit(solution)/shard_map/reshape | solution.py:324
  1.5 0.7 %and_select_fusion = s32[32]{0:T(128)S(1)} fusion(s32[32]{0:T(128)} %param.13), kind=kLoop, calls=%fused_computation.9 | loop fusion | flops 480 | bytes 256 | tf_op jit(solution)/shard_map/jit(floor_divide)/jit(_where)/select_n | solution.py:325
  2.1 0.1 reshape.31
  2.2 0.0 copy-start.3
  2.2 0.1 copy.10
  2.3 0.1 select_reduce_fusion
  2.5 0.0 copy-start.1
  2.5 1.0 %broadcast_in_dim.35 = f32[3,64,16,7]{2,1,3,0:T(8,128)S(1)} broadcast(bf16[3,64,7]{1,2,0:T(8,128)(2,1)} %param.10), dimensions={0,1,3} | broadcast | bytes 88704 | tf_op jit(solution)/shard_map/broadcast_in_dim | solution.py:334
  3.5 0.4 convert_element_type.11
  3.9 0.0 copy-done.3
  3.9 0.1 slice.24
  3.9 0.1 slice.20
  4.0 0.1 pad_maximum_fusion.filt_ref
  4.1 0.0 copy-done
  4.1 0.0 copy-done.1
  4.1 0.0 copy-start.2
  4.1 0.9 %copy-done.2 = bf16[128,1024]{1,0:T(8,128)(2,1)S(1)} copy-done((bf16[128,1024]{1,0:T(8,128)(2,1)S(1)}, bf16[128,1024]{1,0:T(8,128)(2,1)}, u32[]{:S(2)}) %copy-start.2) | copy-done | bytes 262168
  5.1 53.9 %shard_map.94 = (bf16[3,128,1024]{2,1,0:T(8,128)(2,1)S(1)}, f32[8,11,128]{2,1,0:T(8,128)S(1)}) custom-call(s32[8]{0:T(128)S(1)} %get-tuple-element.8.pick_ref, s32[4]{0:T(128)S(1)} %get-tuple-element.7.origin_ref, bf16[128,4096]{1,0:T(8,128)(2,1)S(1)} %bitcast.10, bf16[3,128,1024]{2,1,0:T(8,128)(2,1)S(1)} %copy-done.1, bf16[128,1024]{1,0:T(8,128)(2,1)S(1)} %copy-done.2, ...), custom_call_target="tpu_custom_call" | custom-call | flops 3221225472 | bytes 5242880 | tf_op jit(solution)/shard_map/pallas_call | solution.py:353
  59.1 0.1 rev.4
  59.1 0.6 %broadcast_multiply_fusion = f32[64,128]{1,0:T(8,128)} fusion(f32[64,128]{1,0:T(8,128)S(1)} %rev.4), kind=kLoop, calls=%fused_computation.1 | loop fusion | flops 8192 | bytes 65536 | tf_op jit(solution)/shard_map/mul | solution.py:390
  59.8 0.6 mul.20
  60.4 0.9 %copy.12 = bf16[3,128,1024]{2,1,0:T(8,128)(2,1)} copy(bf16[3,128,1024]{2,1,0:T(8,128)(2,1)S(1)} %get-tuple-element.12) | data formatting | bytes 1572864
  (8 shorter events, 0.1 us)
Async XLA Ops:
  0.6 3.5 %copy-start = (bf16[1,128,4096]{2,1,0:T(8,128)(2,1)S(1)}, bf16[1,128,4096]{2,1,0:T(8,128)(2,1)}, u32[]{:S(2)}) copy-start(bf16[1,128,4096]{2,1,0:T(8,128)(2,1)} %param.9) | copy-start | bytes 3145732
  2.2 1.6 %copy-start.3 = (bf16[64,128]{1,0:T(8,128)(2,1)S(1)}, bf16[64,128]{1,0:T(8,128)(2,1)}, u32[]{:S(2)}) copy-start(bf16[64,128]{1,0:T(8,128)(2,1)} %param.11) | copy-start | bytes 49156
  2.5 1.7 %copy-start.1 = (bf16[3,128,1024]{2,1,0:T(8,128)(2,1)S(1)}, bf16[3,128,1024]{2,1,0:T(8,128)(2,1)}, u32[]{:S(2)}) copy-start(bf16[3,128,1024]{2,1,0:T(8,128)(2,1)} %feat_ref.1) | copy-start | bytes 2359300
  4.1 1.0 %copy-start.2 = (bf16[128,1024]{1,0:T(8,128)(2,1)S(1)}, bf16[128,1024]{1,0:T(8,128)(2,1)}, u32[]{:S(2)}) copy-start(bf16[128,1024]{1,0:T(8,128)(2,1)} %out_grad_ref.1) | copy-start | bytes 786436

commit v5 on v4

--- a/solution.py
+++ b/solution.py
@@ -22,10 +22,10 @@
 
 
 def whole_kernel(
-    n, tp, pick_ref, origin_ref, attn_ref, feat_ref, out_grad_ref, wt_ref, filt_ref, back_ref,
+    n, tp, pick_ref, origin_ref, attn_ref, feat_ref, out_grad_ref, taps_ref, filt_ref, back_ref,
     feat_out, total_ref,
     streams_ref, kv_ref, before_ref, rim_ref, dmix_ref, ds_ref, after_ref,
-    short_ref, flat_ref, part_ref, sums, gathered, head_ref, tail_in,
+    wt_ref, table_ref, short_ref, flat_ref, part_ref, sums, gathered, head_ref, tail_in,
     got, passed, crossed, acc, pieces, stage, landed, rim_in, key_in, mix_in, ext,
     pair_send, pair_recv, cross_send, cross_recv, send, recv, halo_send, halo_recv,
     send1, recv1, send2, recv2,
@@ -100,6 +100,15 @@
             pair(d, r).wait()
             passed[d, r] = (slab_value(other(d), r) + got[d, r].astype(f32)).astype(got.dtype)
             cross(d, r).start()
+    spread = jnp.where(
+        lax.broadcasted_iota(jnp.int32, (width // GROUP, width), 1) // GROUP
+        == lax.broadcasted_iota(jnp.int32, (width // GROUP, width), 0),
+        1.0,
+        0.0,
+    ).astype(taps_ref.dtype)
+    weights = jnp.dot(taps_ref[...], spread, preferred_element_type=f32)
+    for k in range(3):
+        wt_ref[k] = weights[k * taps : (k + 1) * taps]
     rim_hop.wait()
     first = me == 0
     last = me == n - 1
@@ -173,6 +182,16 @@
 
     lax.fori_loop(0, width // chunk, mixed_step, 0)
 
+    def table_step(g, carry):
+        line = jnp.broadcast_to(back_ref[pl.ds(g, 1), :], (long_taps, long_taps))
+        wheel = pltpu.roll(line, 0, 1, stride=1, stride_axis=0)
+        table_ref[g] = jnp.concatenate(
+            [jnp.where(s >= t, wheel, 0.0), jnp.where(s < t, wheel, 0.0)], axis=1
+        ).astype(kv_ref.dtype)
+        return carry
+
+    lax.fori_loop(0, width // GROUP, table_step, 0)
+
     def wait_step(k, carry):
         route(k).wait()
         return carry
@@ -224,13 +243,7 @@
         window = jnp.concatenate([dmix_ref[:, cols], after_ref[:, cols]], axis=0)
         total = jnp.zeros((long_taps, chunk), f32)
         for g in range(near):
-            line = jnp.broadcast_to(
-                back_ref[pl.ds(c * near + g, 1), :], (long_taps, long_taps)
-            )
-            wheel = pltpu.roll(line, 0, 1, stride=1, stride_axis=0)
-            table = jnp.concatenate(
-                [jnp.where(s >= t, wheel, 0.0), jnp.where(s < t, wheel, 0.0)], axis=1
-            ).astype(kind)
+            table = table_ref[c * near + g]
             product = jnp.dot(table, window, preferred_element_type=f32)
             total = jnp.where(owner == g, product, total)
         for k in (1, 2):
@@ -331,7 +344,7 @@
     keyed = jnp.where(everyone == own_index, positions, -1)
     hits = jnp.any(keyed[:, :, None] == slot_ids[None, None, :], axis=1)
     source_of = jnp.sum(jnp.where(hits, device_ids[:, None], 0), axis=0)
-    short_weights = jnp.transpose(jnp.repeat(short_filt, GROUP, axis=1), (0, 2, 1)).astype(f32)
+    short_rows = jnp.transpose(short_filt, (0, 2, 1)).reshape(3 * short_taps, groups)
     filt = med_filt.astype(f32)
     filt_back = jnp.roll(filt[:, ::-1], 1, axis=1)
     tp_count = lax.axis_size("tp")
@@ -360,6 +373,8 @@
         ),
         scratch_shapes=[
             wide, held, held, heads, held, wide, held,
+            pltpu.VMEM((3, short_taps, width), f32),
+            pltpu.VMEM((groups, taps, 2 * taps), half),
             pltpu.VMEM((3 * short_taps, width), f32),
             pltpu.VMEM((ctx_count * share, taps), f32),
             pltpu.VMEM(parts, f32), pltpu.VMEM(parts, f32), pltpu.VMEM(parts, f32),
@@ -380,7 +395,7 @@
         cost_estimate=cost(12 * groups * taps * taps * chunk, 40 * rows * width),
     )(
         send_slot.astype(jnp.int32), source_of.astype(jnp.int32), attn_parts[0], features,
-        out_grad, short_weights, filt_back, filt,
+        out_grad, short_rows, filt_back, filt,
     )
     flat_totals = totals.reshape(-1, taps)
     short_total = flat_totals[groups:used, :groups].reshape(3, short_taps, groups)

time: 61.5 us -> 64.4 us (1.047)
  local copies, waits for them, and re-layouts: 5.04 us -> 7.82 us
    unnamed x9 -> x11, local copies, waits for them, and re-layouts: 1.84 us -> 4.56 us
    slice x3, local copies, waits for them, and re-layouts: 0.16 us -> 1.61 us  [shards(): filt_back = jnp.roll(filt[:, ::-1], 1, axis=1)]
    broadcast_in_dim x1 -> x0, local copies, waits for them, and re-layouts: 1 us -> none  [shards(): jnp.repeat(short_filt, GROUP, axis=1)]
where the time goes in v5:
time: 64.4 us; the launch traced here: 63.9 us
  Pallas kernels  53.9 us (84%)
  local copies, waits for them, and re-layouts  7.82 us (12%)
  other arithmetic  1.54 us (2%)
  between operations  0.69 us (1%)
    pallas_call x1, Pallas kernels, shards(): pl.pallas_call(functools.partial(whole_kernel, ctx_count, tp_count), in_s...  53.9 us
    unnamed x11, local copies, waits for them, and re-layouts  4.56 us
    slice x3, local copies, waits for them, and re-layouts, shards(): filt_back = jnp.roll(filt[:, ::-1], 1, axis=1)  1.61 us

profile of v5, /device:TPU:0, one launch (start us, length us, event | category | flops | bytes accessed | tf_op | source)
XLA Modules:
  0.0 63.9 jit_solution(2579641069340525334)
XLA Ops:
  0.6 0.0 copy-start.2
  0.6 0.8 %reshape.31 = s32[8,4]{1,0:T(8,128)S(1)} reshape(s32[32]{0:T(128)} %param.12) | data formatting | bytes 256 | tf_op jit(solution)/shard_map/reshape | solution.py:337
  1.4 0.7 %and_select_fusion = s32[32]{0:T(128)S(1)} fusion(s32[32]{0:T(128)} %param.13), kind=kLoop, calls=%fused_computation.9 | loop fusion | flops 480 | bytes 256 | tf_op jit(solution)/shard_map/jit(floor_divide)/jit(_where)/select_n | solution.py:338
  2.1 0.1 reshape.32
  2.2 0.1 copy.10
  2.3 0.1 select_reduce_fusion
  2.4 0.8 %slice.24 = f32[64,127]{1,0:T(8,128)S(1)} slice(bf16[64,128]{1,0:T(8,128)(2,1)} %param.11), slice={[0:64], [1:128]} | slice | bytes 65024 | tf_op jit(solution)/shard_map/jit(_roll_static)/slice | solution.py:349
  3.2 0.1 slice.20
  3.3 0.7 %slice.23 = f32[64,1]{1,0:T(8,128)S(1)} slice(bf16[64,128]{1,0:T(8,128)(2,1)} %param.11), slice={[0:64], [0:1]} | slice | bytes 512 | tf_op jit(solution)/shard_map/jit(_roll_static)/slice | solution.py:349
  4.0 0.0 copy-start.3
  4.0 0.1 pad_maximum_fusion.filt_ref
  4.1 0.6 copy-done.3
  4.7 0.0 copy-start.4
  4.8 0.7 %copy-done.4 = bf16[3,64,7]{1,2,0:T(8,128)(2,1)S(1)} copy-done((bf16[3,64,7]{1,2,0:T(8,128)(2,1)S(1)}, bf16[3,64,7]{1,2,0:T(8,128)(2,1)}, u32[]{:S(2)}) %copy-start.4) | copy-done | bytes 2712
  5.5 0.0 copy-done.2
  5.5 0.0 copy-start
  5.5 1.2 %copy-done = bf16[1,128,4096]{2,1,0:T(8,128)(2,1)S(1)} copy-done((bf16[1,128,4096]{2,1,0:T(8,128)(2,1)S(1)}, bf16[1,128,4096]{2,1,0:T(8,128)(2,1)}, u32[]{:S(2)}) %copy-start) | copy-done | bytes 1048600
  6.7 0.0 copy-start.1
  6.7 1.1 %copy-done.1 = bf16[3,128,1024]{2,1,0:T(8,128)(2,1)S(1)} copy-done((bf16[3,128,1024]{2,1,0:T(8,128)(2,1)S(1)}, bf16[3,128,1024]{2,1,0:T(8,128)(2,1)}, u32[]{:S(2)}) %copy-start.1) | copy-done | bytes 786456
  7.8 53.9 %shard_map.94 = (bf16[3,128,1024]{2,1,0:T(8,128)(2,1)S(1)}, f32[8,11,128]{2,1,0:T(8,128)S(1)}) custom-call(s32[8]{0:T(128)S(1)} %get-tuple-element.8.pick_ref, s32[4]{0:T(128)S(1)} %get-tuple-element.7.origin_ref, bf16[128,4096]{1,0:T(8,128)(2,1)S(1)} %bitcast.5, bf16[3,128,1024]{2,1,0:T(8,128)(2,1)S(1)} %copy-done.1, bf16[128,1024]{1,0:T(8,128)(2,1)S(1)} %copy-done.2, ...), custom_call_target="tpu_custom_call" | custom-call | flops 3221225472 | bytes 5242880 | tf_op jit(solution)/shard_map/pallas_call | solution.py:366
  61.7 0.1 rev.4
  61.8 0.6 broadcast_multiply_fusion
  62.4 0.6 mul.20
  63.0 0.9 %copy.12 = bf16[3,128,1024]{2,1,0:T(8,128)(2,1)} copy(bf16[3,128,1024]{2,1,0:T(8,128)(2,1)S(1)} %get-tuple-element.12) | data formatting | bytes 1572864
  (8 shorter events, 0.1 us)
Async XLA Ops:
  0.6 4.8 %copy-start.2 = (bf16[128,1024]{1,0:T(8,128)(2,1)S(1)}, bf16[128,1024]{1,0:T(8,128)(2,1)}, u32[]{:S(2)}) copy-start(bf16[128,1024]{1,0:T(8,128)(2,1)} %out_grad_ref.1) | copy-start | bytes 786436
  4.0 0.7 %copy-start.3 = (bf16[64,128]{1,0:T(8,128)(2,1)S(1)}, bf16[64,128]{1,0:T(8,128)(2,1)}, u32[]{:S(2)}) copy-start(bf16[64,128]{1,0:T(8,128)(2,1)} %param.11) | copy-start | bytes 49156
  4.7 0.7 %copy-start.4 = (bf16[3,64,7]{1,2,0:T(8,128)(2,1)S(1)}, bf16[3,64,7]{1,2,0:T(8,128)(2,1)}, u32[]{:S(2)}) copy-start(bf16[3,64,7]{1,2,0:T(8,128)(2,1)} %param.10) | copy-start | bytes 8068
  5.5 1.2 %copy-start = (bf16[1,128,4096]{2,1,0:T(8,128)(2,1)S(1)}, bf16[1,128,4096]{2,1,0:T(8,128)(2,1)}, u32[]{:S(2)}) copy-start(bf16[1,128,4096]{2,1,0:T(8,128)(2,1)} %param.9) | copy-start | bytes 3145732
  6.7 1.1 %copy-start.1 = (bf16[3,128,1024]{2,1,0:T(8,128)(2,1)S(1)}, bf16[3,128,1024]{2,1,0:T(8,128)(2,1)}, u32[]{:S(2)}) copy-start(bf16[3,128,1024]{2,1,0:T(8,128)(2,1)} %feat_ref.1) | copy-start | bytes 2359300
